TPU v7x, 512 devices: a whole 4x8x8 slice. The times are simulated.
512 devices in a mesh: wide: 64 (over z, y), narrow: 8 (over x, core).
Axes of the slice: x: 4, y: 8, z: 8, core: 2. Of those that a mesh axis runs over, the one named last changes fastest.
Arguments:
- node_latent: bfloat16 [65536, 512], P(('wide', 'narrow')), may hold values from -6 to 6
- edge_latent: bfloat16 [262144, 512], P(('wide', 'narrow')), may hold values from -6 to 6
- node_cotangent: bfloat16 [65536, 512], P(('wide', 'narrow')), may hold values from -6 to 6
- w_first: bfloat16 [1536, 512], replicated, may hold values from -2 to 2
- bias_first: bfloat16 [512], replicated, may hold values from -4 to 4
- w_second: bfloat16 [512, 512], replicated, may hold values from -2 to 2
- bias_second: bfloat16 [512], replicated, may hold values from -4 to 4
- norm_gain: bfloat16 [512], replicated, may hold values from 0.099609375 to 1.8984375
- send_map: int32 [512, 4, 64], P(('wide', 'narrow')), may hold values from -1 to 127, as said below
- edge_sender: int32 [262144], P(('wide', 'narrow')), may hold values from 0 to 383, as said below
- edge_receiver: int32 [262144], P(('wide', 'narrow')), may hold values from 0 to 127
Outputs:
- node_grad: bfloat16 [65536, 512], P(('wide', 'narrow'))
- edge_grad: bfloat16 [262144, 512], P(('wide', 'narrow'))
- first_update: float32 [1536, 512], P('wide')
- second_update: float32 [512, 512], P('wide')
Inputs may be any that keep to these rules, and one draw needn't show every extreme that they name: `send_map`: -1 marks an unused slot; in each row the used slots come first, at most 64, about a third of them on average; in every draw some partition uses all 64 slots toward a wide neighbour; partitions at narrow index 0 send nothing toward block 3 of a lower neighbour and those at the last narrow index nothing toward a higher one. `edge_sender`: a value below 128 is a local node; 128 + k * 64 + s names slot s of received block k, and only slots that the sending partition uses are named.
All inputs are finite; a program needn't handle non-finite values.
Results may differ from a plain program's by a relative error of at most 0.0085.
Values may be sent and summed in bfloat16 or wider, within the bound.
A program may use at most 64 MiB of HBM per device.

v0:
```python
import math

import jax
import jax.numpy as jnp
from jax import lax
from jax.sharding import Mesh
from jax.sharding import PartitionSpec as P

WIDE = ("wide_0", "wide_1")
WIDE_NARROW = ("wide_0", "wide_1", "narrow")


def shifted(value, axis, steps):
    count = lax.axis_size(axis)
    pairs = [(source, (source + steps) % count) for source in range(count)]
    return lax.ppermute(value, axis, pairs)


def shifted_2(block, axis, distance):
    devices = range(lax.axis_size(axis))
    route = [(i - distance, i) for i in devices if i - distance in devices]
    return lax.ppermute(block, axis, route)


def in_blocks(x, dim, count):
    before, after = (x.shape[:dim], x.shape[dim + 1 :])
    return jnp.moveaxis(x.reshape(*before, count, -1, *after), dim, 0)


def summed_on_arrival(x, axis, dim):
    count = lax.axis_size(axis)
    tiles = lax.all_to_all(in_blocks(x, dim, count), axis, 0, 0, tiled=True)
    return jnp.sum(tiles.astype(jnp.float32), axis=0)


def from_everyone(x, axis):
    copies = jnp.broadcast_to(x, (lax.axis_size(axis), *x.shape))
    return lax.all_to_all(copies, axis, split_axis=0, concat_axis=0, tiled=True)


def of_everyone(x, axis):
    everything = from_everyone(x, axis)
    return jnp.sum(everything.astype(jnp.float32), axis=0)


def over_axes(x, axes):
    for axis in axes:
        x = lax.psum(x, axis)
    return x


def neighbours(blocks, direction):
    higher = shifted(blocks[0], WIDE, direction)
    lower = shifted(blocks[1], WIDE, -direction)
    up_side = shifted_2(blocks[2], "narrow", direction)
    down_side = shifted_2(blocks[3], "narrow", -direction)
    return jnp.stack([higher, lower, up_side, down_side], 0)


def norm_parts(second_pre):
    mean_value = jnp.mean(second_pre, -1, keepdims=True)
    centered = second_pre - mean_value
    variance = jnp.mean(centered * centered, -1, keepdims=True)
    inv_std = lax.rsqrt(variance + 1e-05)
    return (centered * inv_std, inv_std)


def clip_share(grad_share, grad_sq, weight_sq, fan_rows):
    unit_ratio = jnp.sqrt((grad_sq + 1e-06) / (weight_sq + 1e-06))
    mean_ratio = jnp.mean(unit_ratio)
    factor = jnp.minimum(
        1.0 / (mean_ratio * jnp.sqrt(weight_sq + 1e-06)), 1.0 / jnp.sqrt(grad_sq + 1e-06)
    )
    return grad_share * factor * math.sqrt(fan_rows)


def edge_contract(hot_table, values):
    return lax.dot_general(
        hot_table,
        values,
        (((0,), (0,)), ((), ())),
        precision=lax.Precision.HIGHEST,
        preferred_element_type=jnp.float32,
    )


def per_device(
    node_latent,
    edge_latent,
    node_cotangent,
    w_first,
    bias_first,
    w_second,
    bias_second,
    norm_gain,
    send_map,
    edge_sender,
    edge_receiver,
):
    node_count, feature_width = node_latent.shape
    halo_slots = send_map.shape[2]
    table_rows = node_count + 4 * halo_slots
    send_hot = (send_map[0][:, :, None] == jnp.arange(node_count, dtype=jnp.int32)).astype(
        jnp.bfloat16
    )
    outgoing = jnp.einsum(
        "khn,nd->khd", send_hot, node_latent, preferred_element_type=jnp.float32
    ).astype(jnp.bfloat16)
    received = neighbours(outgoing, 1)
    node_table = jnp.concatenate([node_latent, received.reshape(4 * halo_slots, feature_width)], 0)
    sender_hot = (edge_sender[:, None] == jnp.arange(table_rows, dtype=jnp.int32)).astype(
        jnp.bfloat16
    )
    receiver_hot = (edge_receiver[:, None] == jnp.arange(node_count, dtype=jnp.int32)).astype(
        jnp.bfloat16
    )
    sender_rows = jnp.dot(sender_hot, node_table, preferred_element_type=jnp.float32).astype(
        jnp.bfloat16
    )
    receiver_rows = jnp.dot(receiver_hot, node_latent, preferred_element_type=jnp.float32).astype(
        jnp.bfloat16
    )
    inputs = jnp.concatenate([edge_latent, sender_rows, receiver_rows], 1)
    preact = jnp.dot(inputs, w_first, preferred_element_type=jnp.float32) + bias_first.astype(
        jnp.float32
    )
    activation = jax.nn.silu(preact).astype(jnp.bfloat16)
    second_pre = jnp.dot(
        activation, w_second, preferred_element_type=jnp.float32
    ) + bias_second.astype(jnp.float32)
    normalized, inv_std = norm_parts(second_pre)
    upstream = jnp.dot(receiver_hot, node_cotangent, preferred_element_type=jnp.float32)
    scaled = upstream * norm_gain.astype(jnp.float32)
    norm_back = (
        inv_std
        * (
            scaled
            - jnp.mean(scaled, -1, keepdims=True)
            - normalized * jnp.mean(scaled * normalized, -1, keepdims=True)
        )
    ).astype(jnp.bfloat16)
    second_grad = lax.dot_general(
        activation, norm_back, (((0,), (0,)), ((), ())), preferred_element_type=jnp.float32
    )
    sigmoid_pre = jax.nn.sigmoid(preact)
    pre_back = (
        jnp.dot(norm_back, w_second.T, preferred_element_type=jnp.float32)
        * sigmoid_pre
        * (1.0 + preact * (1.0 - sigmoid_pre))
    ).astype(jnp.bfloat16)
    first_grad = lax.dot_general(
        inputs, pre_back, (((0,), (0,)), ((), ())), preferred_element_type=jnp.float32
    )
    input_back = jnp.dot(pre_back, w_first.T, preferred_element_type=jnp.float32)
    edge_grad = (upstream + input_back[:, :feature_width]).astype(jnp.bfloat16)
    table_grad = edge_contract(
        sender_hot.astype(jnp.float32), input_back[:, feature_width : 2 * feature_width]
    )
    receiver_grad = edge_contract(
        receiver_hot.astype(jnp.float32), input_back[:, 2 * feature_width :]
    )
    halo_grad = table_grad[node_count:].reshape(4, halo_slots, feature_width).astype(jnp.bfloat16)
    returned = neighbours(halo_grad, -1)
    back = jnp.einsum("khn,khd->nd", send_hot, returned, preferred_element_type=jnp.float32)
    node_grad = (
        node_cotangent.astype(jnp.float32) + table_grad[:node_count] + receiver_grad + back
    ).astype(jnp.bfloat16)
    first_weight_sq = jnp.sum(jnp.square(w_first.astype(jnp.float32)), 0)
    second_weight_sq = jnp.sum(jnp.square(w_second.astype(jnp.float32)), 0)
    first_share, second_share = (
        summed_on_arrival(first_grad.astype(jnp.bfloat16), WIDE, 0),
        summed_on_arrival(second_grad.astype(jnp.bfloat16), WIDE, 0),
    )
    first_share, second_share = (
        of_everyone(first_share.astype(jnp.bfloat16), "narrow").astype(jnp.float32),
        of_everyone(second_share.astype(jnp.bfloat16), "narrow").astype(jnp.float32),
    )
    first_grad_sq, second_grad_sq = (
        over_axes(jnp.sum(first_share * first_share, 0), WIDE),
        over_axes(jnp.sum(second_share * second_share, 0), WIDE),
    )
    first_update = clip_share(first_share, first_grad_sq, first_weight_sq, w_first.shape[0])
    second_update = clip_share(second_share, second_grad_sq, second_weight_sq, w_second.shape[0])
    return (node_grad, edge_grad, first_update, second_update)


def solution(mesh):
    finer = Mesh(mesh.devices.reshape(8, 8, mesh.shape["narrow"]), ("wide_0", "wide_1", "narrow"))
    in_specs = (
        P(WIDE_NARROW, None),
        P(WIDE_NARROW, None),
        P(WIDE_NARROW, None),
        P(),
        P(),
        P(),
        P(),
        P(),
        P(WIDE_NARROW, None, None),
        P(WIDE_NARROW),
        P(WIDE_NARROW),
    )
    out_specs = (P(WIDE_NARROW, None), P(WIDE_NARROW, None), P(WIDE, None), P(WIDE, None))
    return jax.shard_map(
        per_device, mesh=finer, in_specs=in_specs, out_specs=out_specs, check_vma=False
    )
```

profile of v0, /device:TPU:8, one launch (start us, length us, event | category | flops | bytes accessed | tf_op | source)
XLA Modules:
  0.0 163.1 jit_solution(3371856048351125120)
XLA Ops:
  0.7 1.2 convolution_convert_fusion.4
  2.0 3.5 %collective-permute-start = (bf16[64,512]{1,0:T(8,128)(2,1)S(1)}, bf16[64,512]{1,0:T(8,128)(2,1)S(1)}, u32[]{:S(2)}, u32[]{:S(2)}) collective-permute-start(bf16[64,512]{1,0:T(8,128)(2,1)S(1)} %get-tuple-element.22), channel_id=1, source_target_pairs={{0,8},{8,16},{16,24},{24,32},{32,40},{40,48},{48,56},{56,64},{64,7... | collective-permute-start | bytes 196616 | tf_op jit(solution)/shard_map/ppermute | solution.py:16
  5.5 1.3 collective-permute-start.3
  6.8 3.0 %collective-permute-start.2 = (bf16[64,512]{1,0:T(8,128)(2,1)S(1)}, bf16[64,512]{1,0:T(8,128)(2,1)S(1)}, u32[]{:S(2)}, u32[]{:S(2)}) collective-permute-start(bf16[64,512]{1,0:T(8,128)(2,1)S(1)} %get-tuple-element.24), channel_id=1, source_target_pairs={{0,1},{1,2},{2,3},{3,4},{4,5},{5,6},{6,7},{8,9},{9,10},{10,11},{11... | collective-permute-start | bytes 196616 | tf_op jit(solution)/shard_map/ppermute | solution.py:22
  9.8 6.1 %collective-permute-start.1 = (bf16[64,512]{1,0:T(8,128)(2,1)S(1)}, bf16[64,512]{1,0:T(8,128)(2,1)S(1)}, u32[]{:S(2)}, u32[]{:S(2)}) collective-permute-start(bf16[64,512]{1,0:T(8,128)(2,1)S(1)} %get-tuple-element.25), channel_id=1, source_target_pairs={{0,504},{8,0},{16,8},{24,16},{32,24},{40,32},{48,40},{56,48},{64,5... | collective-permute-start | bytes 196616 | tf_op jit(solution)/shard_map/ppermute | solution.py:16
  16.0 1.3 convolution_convert_fusion.3
  17.4 1.0 copy.18
  19.9 1.0 convolution_add_fusion.1
  23.8 1.3 fusion.2
  25.1 14.9 %all-to-all-start.2 = ((bf16[64,8,512]{2,1,0:T(8,128)(2,1)}), bf16[64,8,512]{2,1,0:T(8,128)(2,1)S(1)}, u32[]{:S(2)}, u32[]{:S(2)}) async-start(bf16[64,8,512]{2,1,0:T(8,128)(2,1)} %fusion.2), calls=%async_computation.2 | async-start | bytes 1048576 | tf_op jit(solution)/shard_map/all_to_all | solution.py:32
  40.0 2.1 %fusion.1 = bf16[512,512]{1,0:T(8,128)(2,1)S(1)} fusion(bf16[512,512]{0,1:T(8,128)(2,1)} %copy-done.13, bf16[512,512]{1,0:T(8,128)(2,1)S(1)} %copy-done.10, f32[512,512]{1,0:T(8,128)} %copy-done.23), kind=kOutput, calls=%fused_computation.7 | convolution fusion | flops 270794752 | bytes 2621440 | tf_op jit(solution)/shard_map/dot_general | solution.py:147
  43.0 2.1 %convolution_convert_fusion = bf16[1536,512]{1,0:T(8,128)(2,1)} fusion(bf16[512,512]{1,0:T(8,128)(2,1)S(1)} %fusion.1, bf16[512,512]{0,1:T(8,128)(2,1)S(1)} %convolution_convert_fusion.3, bf16[512,512]{0,1:T(8,128)(2,1)S(1)} %copy-done.22, bf16[512,512]{0,1:T(8,128)(2,1)S(1)} %copy-done.12), kind=kOutput, calls=%fused_computation.1 | convolution fusion | flops 810811392 | bytes 3670016 | tf_op jit(solution)/shard_map/dot_general | solution.py:151
  45.1 14.4 %all-to-all-done.2 = bf16[64,8,512]{2,1,0:T(8,128)(2,1)S(1)} async-done(((bf16[64,8,512]{2,1,0:T(8,128)(2,1)}), bf16[64,8,512]{2,1,0:T(8,128)(2,1)S(1)}, u32[]{:S(2)}, u32[]{:S(2)}) %all-to-all-start.2) | async-done | bytes 524320 | tf_op jit(solution)/shard_map/all_to_all | solution.py:32
  60.3 5.7 %all-to-all-start = ((bf16[64,24,512]{2,1,0:T(8,128)(2,1)}), bf16[64,24,512]{2,1,0:T(8,128)(2,1)}, u32[]{:S(2)}, u32[]{:S(2)}) async-start(bf16[64,24,512]{2,1,0:T(8,128)(2,1)} %bitcast.40), calls=%async_computation | async-start | bytes 3145728 | tf_op jit(solution)/shard_map/all_to_all | solution.py:32
  67.5 1.0 fusion.34
  68.6 1.1 slice.69
  69.6 2.5 %copy.21 = f32[512,512]{0,1:T(8,128)} copy(f32[512,512]{1,0:T(8,128)} %slice.69) | data formatting | bytes 2097152
  73.8 2.5 %collective-permute-start.4 = (bf16[64,512]{1,0:T(8,128)(2,1)}, bf16[64,512]{1,0:T(8,128)(2,1)}, u32[]{:S(2)}, u32[]{:S(2)}) collective-permute-start(bf16[64,512]{1,0:T(8,128)(2,1)} %get-tuple-element.18), channel_id=1, source_target_pairs={{0,504},{8,0},{16,8},{24,16},{32,24},{40,32},{48,40},{56,48},{64,5... | collective-permute-start | bytes 196616 | tf_op jit(solution)/shard_map/ppermute | solution.py:16
  76.3 1.9 %collective-permute-start.7 = (bf16[64,512]{1,0:T(8,128)(2,1)}, bf16[64,512]{1,0:T(8,128)(2,1)}, u32[]{:S(2)}, u32[]{:S(2)}) collective-permute-start(bf16[64,512]{1,0:T(8,128)(2,1)} %get-tuple-element.19), channel_id=1, source_target_pairs={{0,1},{1,2},{2,3},{3,4},{4,5},{5,6},{6,7},{8,9},{9,10},{10,11},{11... | collective-permute-start | bytes 196616 | tf_op jit(solution)/shard_map/ppermute | solution.py:22
  78.3 1.3 collective-permute-start.6
  79.6 3.3 %collective-permute-start.5 = (bf16[64,512]{1,0:T(8,128)(2,1)}, bf16[64,512]{1,0:T(8,128)(2,1)}, u32[]{:S(2)}, u32[]{:S(2)}) collective-permute-start(bf16[64,512]{1,0:T(8,128)(2,1)} %get-tuple-element.21), channel_id=1, source_target_pairs={{0,8},{8,16},{16,24},{24,32},{32,40},{40,48},{48,56},{56,64},{64,7... | collective-permute-start | bytes 196616 | tf_op jit(solution)/shard_map/ppermute | solution.py:16
  84.5 2.0 %copy.20 = bf16[512,512]{1,0:T(8,128)(2,1)} copy(bf16[512,512]{0,1:T(8,128)(2,1)} %add_convert_fusion) | data formatting | bytes 1048576
  86.5 1.1 reduce_sum.141
  87.7 19.0 %all-to-all-done = bf16[64,24,512]{2,1,0:T(8,128)(2,1)} async-done(((bf16[64,24,512]{2,1,0:T(8,128)(2,1)}), bf16[64,24,512]{2,1,0:T(8,128)(2,1)}, u32[]{:S(2)}, u32[]{:S(2)}) %all-to-all-start) | async-done | bytes 1572896 | tf_op jit(solution)/shard_map/all_to_all | solution.py:32
  107.3 3.9 %all-to-all-start.3 = ((bf16[8,8,512]{2,1,0:T(8,128)(2,1)}), bf16[8,8,512]{2,1,0:T(8,128)(2,1)S(1)}, u32[]{:S(2)}, u32[]{:S(2)}) async-start(bf16[8,8,512]{2,1,0:T(8,128)(2,1)} %broadcast_in_dim.5), calls=%async_computation.3 | async-start | bytes 131072 | tf_op jit(solution)/shard_map/all_to_all | solution.py:38
  111.3 1.9 %fusion.4 = bf16[128,512]{1,0:T(8,128)(2,1)} fusion(f32[128,512]{1,0:T(8,128)S(1)} %convolution_add_fusion.2, bf16[1,64,512]{2,1,0:T(8,128)(2,1)} %bitcast.14, bf16[1,64,512]{2,1,0:T(8,128)(2,1)} %bitcast.13, bf16[1,64,512]{2,1,0:T(8,128)(2,1)} %bitcast.12, bf16[1,64,512]{2,1,0:T(8,128)(2,1)} %bitcast.11, s32[4,64]{1,0:T(4,128)S(1)} %bitcast.47), kind=kOutput, calls=%fused_computation.16 | convolution fusion | flops 34111488 | bytes 656384 | tf_op jit(solution)/shard_map/khn,khd->nd/dot_general | solution.py:164
  113.2 1.7 %reduce_sum.136 = bf16[24,512]{1,0:T(8,128)(2,1)S(1)} reduce(bf16[64,24,512]{2,1,0:T(8,128)(2,1)} %all-to-all-done, bf16[]{:T(256)} %constant.23.clone.1), dimensions={0}, to_apply=%region_4.5 | reduce | flops 774144 | bytes 1597442 | tf_op jit(solution)/shard_map/reduce_sum | solution.py:33
  114.9 2.0 %all-to-all-done.3 = bf16[8,8,512]{2,1,0:T(8,128)(2,1)S(1)} async-done(((bf16[8,8,512]{2,1,0:T(8,128)(2,1)}), bf16[8,8,512]{2,1,0:T(8,128)(2,1)S(1)}, u32[]{:S(2)}, u32[]{:S(2)}) %all-to-all-start.3) | async-done | bytes 65568 | tf_op jit(solution)/shard_map/all_to_all | solution.py:38
  117.6 3.4 %all-to-all-start.1 = ((bf16[8,24,512]{2,1,0:T(8,128)(2,1)}), bf16[8,24,512]{2,1,0:T(8,128)(2,1)S(1)}, u32[]{:S(2)}, u32[]{:S(2)}) async-start(bf16[8,24,512]{2,1,0:T(8,128)(2,1)} %broadcast_in_dim.4), calls=%async_computation.1 | async-start | bytes 393216 | tf_op jit(solution)/shard_map/all_to_all | solution.py:38
  121.0 6.7 %all-to-all-done.1 = bf16[8,24,512]{2,1,0:T(8,128)(2,1)S(1)} async-done(((bf16[8,24,512]{2,1,0:T(8,128)(2,1)}), bf16[8,24,512]{2,1,0:T(8,128)(2,1)S(1)}, u32[]{:S(2)}, u32[]{:S(2)}) %all-to-all-start.1) | async-done | bytes 196640 | tf_op jit(solution)/shard_map/all_to_all | solution.py:38
  127.8 15.6 %all-reduce.1 = (f32[512]{0:T(512)S(1)}, f32[512]{0:T(512)S(1)}) all-reduce(f32[512]{0:T(512)S(1)} %multiply_reduce_fusion.5, f32[512]{0:T(512)S(1)} %multiply_reduce_fusion.6), channel_id=1, replica_groups=mesh['wide_0'=8,'wide_1'=8,'narrow'=8] {'wide_0'}, use_global_device_ids=true, to_apply=%region_7.8 | all-reduce | flops 1024 | bytes 8192 | tf_op jit(solution)/shard_map/psum | solution.py:48
  143.4 15.9 %all-reduce = (f32[512]{0:T(512)S(1)}, f32[512]{0:T(512)S(1)}) all-reduce(f32[512]{0:T(512)S(1)} %get-tuple-element.16, f32[512]{0:T(512)S(1)} %get-tuple-element.17), channel_id=1, replica_groups=mesh['wide_0'=8,'wide_1'=8,'narrow'=8] {'wide_1'}, use_global_device_ids=true, to_apply=%region_8.9 | all-reduce | flops 1024 | bytes 8192 | tf_op jit(solution)/shard_map/psum | solution.py:48
  (87 shorter events, 14.5 us)
Async XLA Ops:
  0.6 16.7 %copy-start.18 = (bf16[512]{0:T(512)(128)(2,1)S(1)}, bf16[512]{0:T(512)(128)(2,1)}, u32[]{:S(2)}) copy-start(bf16[512]{0:T(512)(128)(2,1)} %param.18) | copy-start | bytes 3076
  0.6 16.7 %copy-start.19 = (bf16[512]{0:T(512)(128)(2,1)S(1)}, bf16[512]{0:T(512)(128)(2,1)}, u32[]{:S(2)}) copy-start(bf16[512]{0:T(512)(128)(2,1)} %param.15) | copy-start | bytes 3076
  0.7 16.7 %copy-start.20 = (bf16[512]{0:T(512)(128)(2,1)S(1)}, bf16[512]{0:T(512)(128)(2,1)}, u32[]{:S(2)}) copy-start(bf16[512]{0:T(512)(128)(2,1)} %param.17) | copy-start | bytes 3076
  0.7 16.7 %copy-start.9 = (bf16[512,512]{1,0:T(8,128)(2,1)S(1)}, bf16[512,512]{1,0:T(8,128)(2,1)}, u32[]{:S(2)}) copy-start(bf16[512,512]{1,0:T(8,128)(2,1)} %param.12) | copy-start | bytes 1572868
  0.7 17.8 %copy-start.8 = (bf16[128,512]{1,0:T(8,128)(2,1)S(1)}, bf16[128,512]{1,0:T(8,128)(2,1)}, u32[]{:S(2)}) copy-start(bf16[128,512]{1,0:T(8,128)(2,1)} %param.11) | copy-start | bytes 393220
  0.7 17.8 %copy-start.16 = (s32[512]{0:T(512)S(1)}, s32[512]{0:T(512)}, u32[]{:S(2)}) copy-start(s32[512]{0:T(512)} %param.20) | copy-start | bytes 6148
  2.0 16.4 %collective-permute-start = (bf16[64,512]{1,0:T(8,128)(2,1)S(1)}, bf16[64,512]{1,0:T(8,128)(2,1)S(1)}, u32[]{:S(2)}, u32[]{:S(2)}) collective-permute-start(bf16[64,512]{1,0:T(8,128)(2,1)S(1)} %get-tuple-element.22), channel_id=1, source_target_pairs={{0,8},{8,16},{16,24},{24,32},{32,40},{40,48},{48,56},{56,64},{64,7... | collective-permute-start | bytes 196616 | tf_op jit(solution)/shard_map/ppermute | solution.py:16
  5.5 12.9 %collective-permute-start.3 = (bf16[64,512]{1,0:T(8,128)(2,1)S(1)}, bf16[64,512]{1,0:T(8,128)(2,1)S(1)}, u32[]{:S(2)}, u32[]{:S(2)}) collective-permute-start(bf16[64,512]{1,0:T(8,128)(2,1)S(1)} %get-tuple-element.23), channel_id=1, source_target_pairs={{1,0},{2,1},{3,2},{4,3},{5,4},{6,5},{7,6},{9,8},{10,9},{11,10},{12... | collective-permute-start | bytes 196616 | tf_op jit(solution)/shard_map/ppermute | solution.py:22
  6.8 11.6 %collective-permute-start.2 = (bf16[64,512]{1,0:T(8,128)(2,1)S(1)}, bf16[64,512]{1,0:T(8,128)(2,1)S(1)}, u32[]{:S(2)}, u32[]{:S(2)}) collective-permute-start(bf16[64,512]{1,0:T(8,128)(2,1)S(1)} %get-tuple-element.24), channel_id=1, source_target_pairs={{0,1},{1,2},{2,3},{3,4},{4,5},{5,6},{6,7},{8,9},{9,10},{10,11},{11... | collective-permute-start | bytes 196616 | tf_op jit(solution)/shard_map/ppermute | solution.py:22
  9.8 8.6 %collective-permute-start.1 = (bf16[64,512]{1,0:T(8,128)(2,1)S(1)}, bf16[64,512]{1,0:T(8,128)(2,1)S(1)}, u32[]{:S(2)}, u32[]{:S(2)}) collective-permute-start(bf16[64,512]{1,0:T(8,128)(2,1)S(1)} %get-tuple-element.25), channel_id=1, source_target_pairs={{0,504},{8,0},{16,8},{24,16},{32,24},{40,32},{48,40},{56,48},{64,5... | collective-permute-start | bytes 196616 | tf_op jit(solution)/shard_map/ppermute | solution.py:16
  17.3 2.6 %copy-start.2 = (bf16[1536,512]{1,0:T(8,128)(2,1)S(1)}, bf16[1536,512]{1,0:T(8,128)(2,1)}, u32[]{:S(2)}) copy-start(bf16[1536,512]{1,0:T(8,128)(2,1)} %param.14) | copy-start | bytes 4718596
  18.4 1.5 copy-start.11
  19.9 1.0 copy-start.10
  21.0 2.8 %copy-start.23 = (f32[512,512]{1,0:T(8,128)}, f32[512,512]{1,0:T(8,128)S(1)}, u32[]{:S(2)}) copy-start(f32[512,512]{1,0:T(8,128)S(1)} %convolution_add_fusion.1) | copy-start | bytes 3145732
  21.0 1.0 copy-start.14
  21.0 1.0 copy-start.15
  23.8 1.3 copy-start.13
  25.1 34.4 %all-to-all-start.2 = ((bf16[64,8,512]{2,1,0:T(8,128)(2,1)}), bf16[64,8,512]{2,1,0:T(8,128)(2,1)S(1)}, u32[]{:S(2)}, u32[]{:S(2)}) async-start(bf16[64,8,512]{2,1,0:T(8,128)(2,1)} %fusion.2), calls=%async_computation.2 | async-start | bytes 1048576 | tf_op jit(solution)/shard_map/all_to_all | solution.py:32
  40.0 3.0 %copy-start.12 = (bf16[512,512]{0,1:T(8,128)(2,1)S(1)}, bf16[512,512]{0,1:T(8,128)(2,1)}, u32[]{:S(2)}) copy-start(bf16[512,512]{0,1:T(8,128)(2,1)} %copy.18) | copy-start | bytes 1572868
  40.0 2.9 %copy-start.22 = (bf16[512,512]{0,1:T(8,128)(2,1)S(1)}, bf16[512,512]{0,1:T(8,128)(2,1)}, u32[]{:S(2)}) copy-start(bf16[512,512]{0,1:T(8,128)(2,1)} %copy-done.21) | copy-start | bytes 1572868
  60.3 46.4 %all-to-all-start = ((bf16[64,24,512]{2,1,0:T(8,128)(2,1)}), bf16[64,24,512]{2,1,0:T(8,128)(2,1)}, u32[]{:S(2)}, u32[]{:S(2)}) async-start(bf16[64,24,512]{2,1,0:T(8,128)(2,1)} %bitcast.40), calls=%async_computation | async-start | bytes 3145728 | tf_op jit(solution)/shard_map/all_to_all | solution.py:32
  66.0 1.4 copy-start.3
  66.0 1.5 copy-start.7
  72.2 10.7 %copy-start.1 = (f32[512,512]{0,1:T(8,128)S(1)}, f32[512,512]{0,1:T(8,128)}, u32[]{:S(2)}) copy-start(f32[512,512]{0,1:T(8,128)} %copy-done) | copy-start | bytes 3145732
  72.2 10.7 %copy-start.4 = (f32[512,512]{0,1:T(8,128)S(1)}, f32[512,512]{0,1:T(8,128)}, u32[]{:S(2)}) copy-start(f32[512,512]{0,1:T(8,128)} %copy.21) | copy-start | bytes 3145732
  73.8 37.4 %collective-permute-start.4 = (bf16[64,512]{1,0:T(8,128)(2,1)}, bf16[64,512]{1,0:T(8,128)(2,1)}, u32[]{:S(2)}, u32[]{:S(2)}) collective-permute-start(bf16[64,512]{1,0:T(8,128)(2,1)} %get-tuple-element.18), channel_id=1, source_target_pairs={{0,504},{8,0},{16,8},{24,16},{32,24},{40,32},{48,40},{56,48},{64,5... | collective-permute-start | bytes 196616 | tf_op jit(solution)/shard_map/ppermute | solution.py:16
  76.3 34.9 %collective-permute-start.7 = (bf16[64,512]{1,0:T(8,128)(2,1)}, bf16[64,512]{1,0:T(8,128)(2,1)}, u32[]{:S(2)}, u32[]{:S(2)}) collective-permute-start(bf16[64,512]{1,0:T(8,128)(2,1)} %get-tuple-element.19), channel_id=1, source_target_pairs={{0,1},{1,2},{2,3},{3,4},{4,5},{5,6},{6,7},{8,9},{9,10},{10,11},{11... | collective-permute-start | bytes 196616 | tf_op jit(solution)/shard_map/ppermute | solution.py:22
  78.3 33.0 %collective-permute-start.6 = (bf16[64,512]{1,0:T(8,128)(2,1)}, bf16[64,512]{1,0:T(8,128)(2,1)}, u32[]{:S(2)}, u32[]{:S(2)}) collective-permute-start(bf16[64,512]{1,0:T(8,128)(2,1)} %get-tuple-element.20), channel_id=1, source_target_pairs={{1,0},{2,1},{3,2},{4,3},{5,4},{6,5},{7,6},{9,8},{10,9},{11,10},{12... | collective-permute-start | bytes 196616 | tf_op jit(solution)/shard_map/ppermute | solution.py:22
  79.6 31.7 %collective-permute-start.5 = (bf16[64,512]{1,0:T(8,128)(2,1)}, bf16[64,512]{1,0:T(8,128)(2,1)}, u32[]{:S(2)}, u32[]{:S(2)}) collective-permute-start(bf16[64,512]{1,0:T(8,128)(2,1)} %get-tuple-element.21), channel_id=1, source_target_pairs={{0,8},{8,16},{16,24},{24,32},{32,40},{40,48},{48,56},{56,64},{64,7... | collective-permute-start | bytes 196616 | tf_op jit(solution)/shard_map/ppermute | solution.py:16
  83.9 27.4 %copy-start.17 = (s32[1,4,64]{2,1,0:T(4,128)S(1)}, s32[1,4,64]{2,1,0:T(4,128)}, u32[]{:S(2)}) copy-start(s32[1,4,64]{2,1,0:T(4,128)} %param.19) | copy-start | bytes 3076
  107.3 9.6 %all-to-all-start.3 = ((bf16[8,8,512]{2,1,0:T(8,128)(2,1)}), bf16[8,8,512]{2,1,0:T(8,128)(2,1)S(1)}, u32[]{:S(2)}, u32[]{:S(2)}) async-start(bf16[8,8,512]{2,1,0:T(8,128)(2,1)} %broadcast_in_dim.5), calls=%async_computation.3 | async-start | bytes 131072 | tf_op jit(solution)/shard_map/all_to_all | solution.py:38
  117.6 10.1 %all-to-all-start.1 = ((bf16[8,24,512]{2,1,0:T(8,128)(2,1)}), bf16[8,24,512]{2,1,0:T(8,128)(2,1)S(1)}, u32[]{:S(2)}, u32[]{:S(2)}) async-start(bf16[8,24,512]{2,1,0:T(8,128)(2,1)} %broadcast_in_dim.4), calls=%async_computation.1 | async-start | bytes 393216 | tf_op jit(solution)/shard_map/all_to_all | solution.py:38
  (4 other events, 3.4 us)
where the time goes:
time: 164 us; the launch traced here: 163 us
  starting transfers between devices  50.9 us (31%)
  waiting for transfers between devices  42.1 us (26%)
  blocking collectives  31.6 us (19%)
  matrix products  15.3 us (9%)
  local copies, waits for them, and re-layouts  13.3 us (8%)
  other arithmetic  7.42 us (5%)
  between operations  2.44 us (1%)
    all_to_all x2, waiting for transfers between devices, summed_on_arrival(): tiles = lax.all_to_all(in_blocks(x, dim, count), axis, 0, 0, tiled=True)  33.4 us
    psum x2, blocking collectives, over_axes(): x = lax.psum(x, axis)  31.6 us
    all_to_all x2, starting transfers between devices, summed_on_arrival(): tiles = lax.all_to_all(in_blocks(x, dim, count), axis, 0, 0, tiled=True)  20.6 us
    ppermute x4, starting transfers between devices, shifted(): return lax.ppermute(value, axis, pairs)  15.5 us
    unnamed x51, local copies, waits for them, and re-layouts  10.2 us
    all_to_all x2, waiting for transfers between devices, from_everyone(): return lax.all_to_all(copies, axis, split_axis=0, concat_axis=0, tiled=True)  8.72 us
    ppermute x4, starting transfers between devices, shifted_2(): return lax.ppermute(block, axis, route)  7.53 us
    all_to_all x2, starting transfers between devices, from_everyone(): return lax.all_to_all(copies, axis, split_axis=0, concat_axis=0, tiled=True)  7.34 us
  transfers between devices with their start and end apart: 12, of which 4 were waited for; matrix products, arithmetic and copies ran while one was open for 14% of the time, Pallas kernels for 0%

commit v1 on v0

--- a/solution.py
+++ b/solution.py
@@ -4,10 +4,13 @@
 import jax.numpy as jnp
 from jax import lax
 from jax.sharding import Mesh
+from jax.experimental import pallas as pl
+from jax.experimental.pallas import tpu as pltpu
 from jax.sharding import PartitionSpec as P
 
-WIDE = ("wide_0", "wide_1")
-WIDE_NARROW = ("wide_0", "wide_1", "narrow")
+WIDE = ("z", "y")
+NARROW = ("x", "c")
+WIDE_NARROW = ("z", "y", "x", "c")
 
 
 def shifted(value, axis, steps):
@@ -22,38 +25,11 @@
     return lax.ppermute(block, axis, route)
 
 
-def in_blocks(x, dim, count):
-    before, after = (x.shape[:dim], x.shape[dim + 1 :])
-    return jnp.moveaxis(x.reshape(*before, count, -1, *after), dim, 0)
-
-
-def summed_on_arrival(x, axis, dim):
-    count = lax.axis_size(axis)
-    tiles = lax.all_to_all(in_blocks(x, dim, count), axis, 0, 0, tiled=True)
-    return jnp.sum(tiles.astype(jnp.float32), axis=0)
-
-
-def from_everyone(x, axis):
-    copies = jnp.broadcast_to(x, (lax.axis_size(axis), *x.shape))
-    return lax.all_to_all(copies, axis, split_axis=0, concat_axis=0, tiled=True)
-
-
-def of_everyone(x, axis):
-    everything = from_everyone(x, axis)
-    return jnp.sum(everything.astype(jnp.float32), axis=0)
-
-
-def over_axes(x, axes):
-    for axis in axes:
-        x = lax.psum(x, axis)
-    return x
-
-
 def neighbours(blocks, direction):
     higher = shifted(blocks[0], WIDE, direction)
     lower = shifted(blocks[1], WIDE, -direction)
-    up_side = shifted_2(blocks[2], "narrow", direction)
-    down_side = shifted_2(blocks[3], "narrow", -direction)
+    up_side = shifted_2(blocks[2], NARROW, direction)
+    down_side = shifted_2(blocks[3], NARROW, -direction)
     return jnp.stack([higher, lower, up_side, down_side], 0)
 
 
@@ -63,15 +39,6 @@
     variance = jnp.mean(centered * centered, -1, keepdims=True)
     inv_std = lax.rsqrt(variance + 1e-05)
     return (centered * inv_std, inv_std)
-
-
-def clip_share(grad_share, grad_sq, weight_sq, fan_rows):
-    unit_ratio = jnp.sqrt((grad_sq + 1e-06) / (weight_sq + 1e-06))
-    mean_ratio = jnp.mean(unit_ratio)
-    factor = jnp.minimum(
-        1.0 / (mean_ratio * jnp.sqrt(weight_sq + 1e-06)), 1.0 / jnp.sqrt(grad_sq + 1e-06)
-    )
-    return grad_share * factor * math.sqrt(fan_rows)
 
 
 def edge_contract(hot_table, values):
@@ -82,6 +49,264 @@
         precision=lax.Precision.HIGHEST,
         preferred_element_type=jnp.float32,
     )
+
+
+MESH = pl.DeviceIdType.MESH
+F32 = jnp.float32
+BF16 = jnp.bfloat16
+
+
+class Comm:
+    def __init__(self, send_sems, recv_sems):
+        self.send_sems, self.recv_sems, self.used, self.started = send_sems, recv_sems, 0, []
+
+    def copy(self, src, dst, to):
+        copy = pltpu.make_async_remote_copy(
+            src_ref=src,
+            dst_ref=dst,
+            send_sem=self.send_sems.at[self.used],
+            recv_sem=self.recv_sems.at[self.used],
+            device_id=to,
+            device_id_type=MESH,
+        )
+        self.used += 1
+        self.started.append(copy)
+        copy.start()
+        return copy
+
+    def drain(self):
+        for copy in self.started:
+            copy.wait_send()
+
+
+class Ring:
+    def __init__(self, comm, axis, total, slots):
+        self.comm, self.axis, self.total = comm, axis, total
+        self.count, self.me = lax.axis_size(axis), lax.axis_index(axis)
+        self.half = total.shape[1] // 2
+        self.chains = []
+        used = 0
+        for half in (0, 1):
+            for sign in (-1, 1):
+                hops = self.count // 2 - (0 if (sign < 0) == (half == 0) else 1)
+                self.chains.append((half, sign, hops, slots.at[pl.ds(used, max(hops, 1))]))
+                used += hops
+        self.last = [None] * 4
+
+    def part(self, owner, half):
+        return self.total.at[owner, pl.ds(half * self.half, self.half)]
+
+    def step(self, step):
+        for i, (half, sign, hops, slots) in enumerate(self.chains):
+            if step >= hops:
+                continue
+            owner = lax.rem(self.me + sign * (hops - step) + self.count, self.count)
+            mine = self.part(owner, half)
+            if step:
+                self.last[i].wait_recv()
+                mine[...] = (mine[...].astype(F32) + slots[step - 1].astype(F32)).astype(BF16)
+            to = lax.rem(self.me + sign + self.count, self.count)
+            self.last[i] = self.comm.copy(mine, slots.at[step], {self.axis: to})
+
+    def finish(self, out):
+        for half in (0, 1):
+            here = self.part(self.me, half)
+            value = here[...].astype(F32)
+            for i, (chain_half, _, hops, slots) in enumerate(self.chains):
+                if chain_half == half and hops:
+                    self.last[i].wait_recv()
+                    value = value + slots[hops - 1].astype(F32)
+            out[pl.ds(half * self.half, self.half)] = value.astype(BF16)
+
+
+def scatter(comm, axis, parts, slots):
+    count, me = lax.axis_size(axis), lax.axis_index(axis)
+    copies = []
+    for k in range(1, count):
+        peer = lax.rem(me + k, count)
+        copies.append(comm.copy(parts(peer), slots.at[k - 1], {axis: peer}))
+    return copies
+
+
+def entry_barrier():
+    barrier = pltpu.get_barrier_semaphore()
+    signals = 0
+    for axis in ("z", "y"):
+        count, me = lax.axis_size(axis), lax.axis_index(axis)
+        for k in range(1, count):
+            pl.semaphore_signal(barrier, 1, device_id={axis: lax.rem(me + k, count)}, device_id_type=MESH)
+            signals += 1
+    for device in others_nearby():
+        pl.semaphore_signal(barrier, 1, device_id=device[1], device_id_type=MESH)
+        signals += 1
+    pl.semaphore_wait(barrier, signals)
+
+
+def others_nearby():
+    across, cores = lax.axis_size("x"), lax.axis_size("c")
+    x, c = lax.axis_index("x"), lax.axis_index("c")
+    found = []
+    for k in range(1, across * cores):
+        to_x, to_c = lax.rem(x + k // cores, across), lax.rem(c + k % cores, cores)
+        found.append((k, {"x": to_x, "c": to_c}))
+    return found
+
+
+def clip_rows(grad_sq, weight_sq, which):
+    ratio = jnp.sqrt((grad_sq + 1e-06) / (weight_sq + 1e-06))
+    rows = lax.broadcasted_iota(jnp.int32, ratio.shape, 0)
+    mine = lax.rem(rows, 2) == which
+    mean_ratio = jnp.sum(jnp.where(mine, ratio, 0.0)) / (ratio.shape[0] // 2 * ratio.shape[1])
+    return jnp.minimum(1.0 / (mean_ratio * jnp.sqrt(weight_sq + 1e-06)), 1.0 / jnp.sqrt(grad_sq + 1e-06))
+
+
+def reduce_kernel(
+    grads_a,
+    grads_b,
+    weight_sq,
+    first_out,
+    second_out,
+    from_core_a,
+    from_core_b,
+    total_a,
+    total_b,
+    ring_a,
+    ring_b,
+    over_a,
+    over_b,
+    cross_a,
+    cross_b,
+    share,
+    shares,
+    squares,
+    squares_in,
+    send_sems,
+    recv_sems,
+):
+    comm = Comm(send_sems, recv_sems)
+    c = lax.axis_index("c")
+    nz, ny, across = lax.axis_size("z"), lax.axis_size("y"), lax.axis_size("x")
+    entry_barrier()
+    other = 1 - c
+    pair_a = comm.copy(grads_a.at[other], from_core_a, {"c": other})
+    pair_b = comm.copy(grads_b.at[other], from_core_b, {"c": other})
+    for pair, grads, arrived, total in (
+        (pair_a, grads_a, from_core_a, total_a),
+        (pair_b, grads_b, from_core_b, total_b),
+    ):
+        pair.wait_recv()
+
+        def add(i, _, grads=grads, arrived=arrived, total=total):
+            total[i] = (grads[c, i].astype(F32) + arrived[i].astype(F32)).astype(BF16)
+            return 0
+
+        lax.fori_loop(0, total.shape[0], add, 0)
+    rings = (Ring(comm, "y", total_a, ring_a), Ring(comm, "z", total_b, ring_b))
+    for step in range(max(nz, ny) // 2):
+        for ring in rings:
+            ring.step(step)
+    rings[0].finish(over_a)
+    to_z = scatter(comm, "z", lambda peer: over_a.at[peer], cross_a)
+    rings[1].finish(over_b)
+    to_y = scatter(comm, "y", lambda peer: over_b.at[peer], cross_b)
+    for i, (axis, copies, over, cross) in enumerate(
+        (("z", to_z, over_a, cross_a), ("y", to_y, over_b, cross_b))
+    ):
+        value = over[lax.axis_index(axis)].astype(F32)
+        for k, copy in enumerate(copies):
+            copy.wait_recv()
+            value = value + cross[k].astype(F32)
+        share[i] = value.astype(BF16)
+    here = lax.axis_index("x") * 2 + c
+    shares[here] = share[...]
+    copies = [comm.copy(share, shares.at[here], device) for _, device in others_nearby()]
+    for copy in copies:
+        copy.wait_recv()
+    slabs = []
+    for core in (0, 1):
+        for i in (0, 1):
+            value = shares[core, i].astype(F32)
+            for x in range(1, across):
+                value = value + shares[2 * x + core, i].astype(F32)
+            slabs.append(value)
+    first_rows = first_out.shape[0]
+    sums = []
+    for value in slabs:
+        square = value * value
+        sums.append(jnp.sum(square[:first_rows], 0, keepdims=True))
+        sums.append(jnp.sum(square[first_rows:], 0, keepdims=True))
+    squares[0] = jnp.concatenate(sums, 0)
+    copies = scatter(comm, "y", lambda peer: squares.at[0], squares_in.at[pl.ds(0, ny - 1)])
+    value = squares[0]
+    for k, copy in enumerate(copies):
+        copy.wait_recv()
+        value = value + squares_in[k]
+    squares[1] = value
+    copies = scatter(comm, "z", lambda peer: squares.at[1], squares_in.at[pl.ds(ny - 1, nz - 1)])
+    for k, copy in enumerate(copies):
+        copy.wait_recv()
+        value = value + squares_in[ny - 1 + k]
+    factors = [clip_rows(value, weight_sq[...], which) for which in (0, 1)]
+    for i, slab in enumerate(slabs):
+        columns = pl.ds(128 * i, 128)
+        first = factors[0][2 * i : 2 * i + 1] * math.sqrt(first_rows * nz * ny)
+        second = factors[1][2 * i + 1 : 2 * i + 2] * math.sqrt(second_out.shape[0] * nz * ny)
+        first_out[:, columns] = slab[:first_rows] * first
+        second_out[:, columns] = slab[first_rows:] * second
+    comm.drain()
+
+
+def reduce_updates(first_grad, second_grad, w_first, w_second):
+    nz, ny, across = lax.axis_size("z"), lax.axis_size("y"), lax.axis_size("x")
+    shards = nz * ny
+    rows = (first_grad.shape[0] + second_grad.shape[0]) // shards
+    first_rows, second_rows = first_grad.shape[0] // shards, second_grad.shape[0] // shards
+    blocks = jnp.concatenate(
+        [
+            first_grad.astype(BF16).reshape(nz, ny, first_rows, 2, 2, 128),
+            second_grad.astype(BF16).reshape(nz, ny, second_rows, 2, 2, 128),
+        ],
+        2,
+    )
+    grads_a = jnp.transpose(blocks[:, :, :, :, 0], (3, 1, 0, 2, 4))
+    grads_b = jnp.transpose(blocks[:, :, :, :, 1], (3, 0, 1, 2, 4))
+    weight_sq = jnp.stack(
+        [
+            jnp.sum(jnp.square(w_first.astype(F32)), 0).reshape(4, 128),
+            jnp.sum(jnp.square(w_second.astype(F32)), 0).reshape(4, 128),
+        ],
+        1,
+    ).reshape(8, 128)
+    vmem = pl.BlockSpec(memory_space=pltpu.VMEM)
+    copies = 2 + 2 * 2 * (ny - 1 + nz - 1) + 2 * (nz - 1 + ny - 1) + 2 * across - 1
+    return pl.pallas_call(
+        reduce_kernel,
+        out_shape=(
+            jax.ShapeDtypeStruct((first_rows, 512), F32),
+            jax.ShapeDtypeStruct((second_rows, 512), F32),
+        ),
+        in_specs=[vmem] * 3,
+        out_specs=(vmem, vmem),
+        scratch_shapes=[
+            pltpu.VMEM((ny, nz, rows, 128), BF16),
+            pltpu.VMEM((nz, ny, rows, 128), BF16),
+            pltpu.VMEM((ny, nz, rows, 128), BF16),
+            pltpu.VMEM((nz, ny, rows, 128), BF16),
+            pltpu.VMEM((2 * (ny - 1), nz // 2, rows, 128), BF16),
+            pltpu.VMEM((2 * (nz - 1), ny // 2, rows, 128), BF16),
+            pltpu.VMEM((nz, rows, 128), BF16),
+            pltpu.VMEM((ny, rows, 128), BF16),
+            pltpu.VMEM((nz - 1, rows, 128), BF16),
+            pltpu.VMEM((ny - 1, rows, 128), BF16),
+            pltpu.VMEM((2, rows, 128), BF16),
+            pltpu.VMEM((2 * across, 2, rows, 128), BF16),
+            pltpu.VMEM((2, 8, 128), F32),
+            pltpu.VMEM((ny - 1 + nz - 1, 8, 128), F32),
+            pltpu.SemaphoreType.DMA((copies,)),
+            pltpu.SemaphoreType.DMA((copies,)),
+        ],
+        compiler_params=pltpu.CompilerParams(collective_id=0, has_side_effects=True, vmem_limit_bytes=32 << 20),
+    )(grads_a, grads_b, weight_sq)
 
 
 def per_device(
@@ -165,27 +390,12 @@
     node_grad = (
         node_cotangent.astype(jnp.float32) + table_grad[:node_count] + receiver_grad + back
     ).astype(jnp.bfloat16)
-    first_weight_sq = jnp.sum(jnp.square(w_first.astype(jnp.float32)), 0)
-    second_weight_sq = jnp.sum(jnp.square(w_second.astype(jnp.float32)), 0)
-    first_share, second_share = (
-        summed_on_arrival(first_grad.astype(jnp.bfloat16), WIDE, 0),
-        summed_on_arrival(second_grad.astype(jnp.bfloat16), WIDE, 0),
-    )
-    first_share, second_share = (
-        of_everyone(first_share.astype(jnp.bfloat16), "narrow").astype(jnp.float32),
-        of_everyone(second_share.astype(jnp.bfloat16), "narrow").astype(jnp.float32),
-    )
-    first_grad_sq, second_grad_sq = (
-        over_axes(jnp.sum(first_share * first_share, 0), WIDE),
-        over_axes(jnp.sum(second_share * second_share, 0), WIDE),
-    )
-    first_update = clip_share(first_share, first_grad_sq, first_weight_sq, w_first.shape[0])
-    second_update = clip_share(second_share, second_grad_sq, second_weight_sq, w_second.shape[0])
+    first_update, second_update = reduce_updates(first_grad, second_grad, w_first, w_second)
     return (node_grad, edge_grad, first_update, second_update)
 
 
 def solution(mesh):
-    finer = Mesh(mesh.devices.reshape(8, 8, mesh.shape["narrow"]), ("wide_0", "wide_1", "narrow"))
+    finer = Mesh(mesh.devices.reshape(8, 8, 4, 2), WIDE_NARROW)
     in_specs = (
         P(WIDE_NARROW, None),
         P(WIDE_NARROW, None),

time: 164 us -> 107 us (0.65)
  the two profiles are of different devices: /device:TPU:8 before, /device:TPU:1 now
where the time goes in v1:
time: 107 us
  Pallas kernels  42.3 us (40%)
  starting transfers between devices  32.9 us (31%)
  matrix products  13.4 us (13%)
  local copies, waits for them, and re-layouts  11.1 us (10%)
  other arithmetic  6.06 us (6%)
    pallas_call x1, Pallas kernels, reduce_updates(): pl.pallas_call(reduce_kernel, out_shape=(jax.ShapeDtypeStruct((first_rows...  42.3 us
    ppermute x4, starting transfers between devices, shifted(): return lax.ppermute(value, axis, pairs)  18.9 us
    ppermute x4, starting transfers between devices, shifted_2(): return lax.ppermute(block, axis, route)  14 us
    unnamed x32, local copies, waits for them, and re-layouts  5.8 us
    dot_general x2, matrix products, edge_contract(): lax.dot_general(hot_table, values, (((0,), (0,)), ((), ())), precision=la...  3.72 us
    reshape x1, local copies, waits for them, and re-layouts, reduce_updates(): first_grad.astype(BF16).reshape(nz, ny, first_rows, 2, 2, 128)  2.36 us
  transfers between devices with their start and end apart: 8, of which 0 were waited for; matrix products, arithmetic and copies ran while one was open for 8% of the time, Pallas kernels for 40%

profile of v1, /device:TPU:1, one launch (start us, length us, event | category | flops | bytes accessed | tf_op | source)
XLA Modules:
  0.0 106.9 jit_solution(7520457709556876586)
XLA Ops:
  0.7 1.3 %convolution_convert_fusion.4 = bf16[4,64,512]{2,1,0:T(8,128)(2,1)S(1)} fusion(bf16[128,512]{1,0:T(8,128)(2,1)} %param.11, s32[4,64]{1,0:T(4,128)} %bitcast.58), kind=kOutput, calls=%fused_computation.12 | convolution fusion | flops 33718272 | bytes 394240 | tf_op jit(solution)/shard_map/khn,nd->khd/dot_general | solution.py:331
  2.0 4.0 %collective-permute-start = (bf16[64,512]{1,0:T(8,128)(2,1)S(1)}, bf16[64,512]{1,0:T(8,128)(2,1)S(1)}, u32[]{:S(2)}, u32[]{:S(2)}) collective-permute-start(bf16[64,512]{1,0:T(8,128)(2,1)S(1)} %get-tuple-element.24), channel_id=1, source_target_pairs={{0,8},{8,16},{16,24},{24,32},{32,40},{40,48},{48,56},{56,64},{64,7... | collective-permute-start | bytes 196616 | tf_op jit(solution)/shard_map/ppermute | solution.py:19
  6.0 6.6 %collective-permute-start.3 = (bf16[64,512]{1,0:T(8,128)(2,1)S(1)}, bf16[64,512]{1,0:T(8,128)(2,1)S(1)}, u32[]{:S(2)}, u32[]{:S(2)}) collective-permute-start(bf16[64,512]{1,0:T(8,128)(2,1)S(1)} %get-tuple-element.25), channel_id=1, source_target_pairs={{1,0},{2,1},{3,2},{4,3},{5,4},{6,5},{7,6},{9,8},{10,9},{11,10},{12... | collective-permute-start | bytes 196616 | tf_op jit(solution)/shard_map/ppermute | solution.py:25
  12.7 1.9 %collective-permute-start.2 = (bf16[64,512]{1,0:T(8,128)(2,1)S(1)}, bf16[64,512]{1,0:T(8,128)(2,1)S(1)}, u32[]{:S(2)}, u32[]{:S(2)}) collective-permute-start(bf16[64,512]{1,0:T(8,128)(2,1)S(1)} %get-tuple-element.26), channel_id=1, source_target_pairs={{0,1},{1,2},{2,3},{3,4},{4,5},{5,6},{6,7},{8,9},{9,10},{10,11},{11... | collective-permute-start | bytes 196616 | tf_op jit(solution)/shard_map/ppermute | solution.py:25
  14.6 9.3 %collective-permute-start.1 = (bf16[64,512]{1,0:T(8,128)(2,1)S(1)}, bf16[64,512]{1,0:T(8,128)(2,1)S(1)}, u32[]{:S(2)}, u32[]{:S(2)}) collective-permute-start(bf16[64,512]{1,0:T(8,128)(2,1)S(1)} %get-tuple-element.27), channel_id=1, source_target_pairs={{0,504},{8,0},{16,8},{24,16},{32,24},{40,32},{48,40},{56,48},{64,5... | collective-permute-start | bytes 196616 | tf_op jit(solution)/shard_map/ppermute | solution.py:19
  23.9 0.7 convert_element_type.62
  24.6 0.7 convert_element_type.59
  25.3 0.7 convert_element_type.61
  26.0 1.8 %multiply_reduce_fusion = f32[512]{0:T(512)S(1)} fusion(bf16[1536,512]{1,0:T(8,128)(2,1)} %param.14), kind=kLoop, calls=%fused_computation | loop fusion | flops 2358784 | bytes 1574912 | tf_op jit(solution)/shard_map/reduce_sum | solution.py:275
  28.0 1.0 copy.19
  29.5 0.6 convolution_convert_fusion.2
  30.2 1.0 convolution_add_fusion.1
  32.9 0.7 fusion.1
  34.1 2.1 %convolution_convert_fusion = bf16[1536,512]{1,0:T(8,128)(2,1)} fusion(bf16[512,512]{1,0:T(8,128)(2,1)S(1)} %fusion.1, bf16[512,512]{0,1:T(8,128)(2,1)S(1)} %convolution_convert_fusion.3, bf16[512,512]{0,1:T(8,128)(2,1)S(1)} %convolution_convert_fusion.2, bf16[512,512]{0,1:T(8,128)(2,1)S(1)} %copy-done.7), kind=kOutput, calls=%fused_computation.1 | convolution fusion | flops 810811392 | bytes 3670016 | tf_op jit(solution)/shard_map/dot_general | solution.py:376
  36.2 1.0 fusion.33
  37.2 1.2 %slice.77 = f32[512,512]{1,0:T(8,128)} slice(f32[512,1536]{1,0:T(8,128)S(1)} %fusion.33), slice={[0:512], [0:512]} | slice | bytes 2097152 | tf_op jit(solution)/shard_map/slice | solution.py:380
  38.4 0.8 copy-done
  39.2 1.9 %fusion.32 = (bf16[384,512]{1,0:T(8,128)(2,1)S(1)}, f32[384,512]{1,0:T(8,128)}) fusion(f32[512,1536]{1,0:T(8,128)S(1)} %fusion.33, s32[512]{0:T(512)S(1)} %copy-done.11), kind=kOutput, calls=%fused_computation.70 | convolution fusion | flops 1208352768 | bytes 2230272 | tf_op jit(solution)/shard_map/dot_general | solution.py:45
  41.0 2.4 %reshape.57 = bf16[8,8,24,2,2,128]{5,4,3,2,1,0:T(2,128)(2,1)S(1)} reshape(bf16[1536,512]{1,0:T(8,128)(2,1)} %convolution_convert_fusion) | data formatting | bytes 3145728 | tf_op jit(solution)/shard_map/reshape | solution.py:266
  44.0 1.4 %slice_bitcast_fusion = (bf16[2,8,8,32,128]{4,3,2,1,0:T(8,128)(2,1)S(1)}, bf16[2,8,8,32,128]{4,3,1,2,0:T(8,128)(2,1)}) fusion(bf16[8,8,32,2,2,128]{5,2,1,0,3,4:T(8,128)(2,1)S(1)} %copy_dynamic-update-slice_fusion.1), kind=kLoop, calls=%fused_computation.17 | loop fusion | bytes 4194304 | tf_op jit(solution)/shard_map/transpose | solution.py:272
  45.4 1.3 %copy.25 = f32[512,512]{0,1:T(8,128)} copy(f32[512,512]{1,0:T(8,128)S(1)} %copy-done.2) | data formatting | bytes 2097152
  46.7 1.5 %add_convert_fusion = bf16[512,512]{0,1:T(8,128)(2,1)S(1)} fusion(f32[512,512]{0,1:T(8,128)S(1)} %get-tuple-element.30, f32[512,512]{0,1:T(8,128)} %copy.25), kind=kLoop, calls=%fused_computation.23 | loop fusion | flops 524288 | bytes 2621440 | tf_op jit(solution)/shard_map/convert_element_type | solution.py:380
  48.2 3.7 %collective-permute-start.4 = (bf16[64,512]{1,0:T(8,128)(2,1)S(1)}, bf16[64,512]{1,0:T(8,128)(2,1)S(1)}, u32[]{:S(2)}, u32[]{:S(2)}) collective-permute-start(bf16[64,512]{1,0:T(8,128)(2,1)S(1)} %get-tuple-element.20), channel_id=1, source_target_pairs={{0,504},{8,0},{16,8},{24,16},{32,24},{40,32},{48,40},{56,48},{64,5... | collective-permute-start | bytes 196616 | tf_op jit(solution)/shard_map/ppermute | solution.py:19
  51.9 3.5 %collective-permute-start.7 = (bf16[64,512]{1,0:T(8,128)(2,1)S(1)}, bf16[64,512]{1,0:T(8,128)(2,1)S(1)}, u32[]{:S(2)}, u32[]{:S(2)}) collective-permute-start(bf16[64,512]{1,0:T(8,128)(2,1)S(1)} %get-tuple-element.21), channel_id=1, source_target_pairs={{0,1},{1,2},{2,3},{3,4},{4,5},{5,6},{6,7},{8,9},{9,10},{10,11},{11... | collective-permute-start | bytes 196616 | tf_op jit(solution)/shard_map/ppermute | solution.py:25
  55.4 1.9 %collective-permute-start.6 = (bf16[64,512]{1,0:T(8,128)(2,1)S(1)}, bf16[64,512]{1,0:T(8,128)(2,1)S(1)}, u32[]{:S(2)}, u32[]{:S(2)}) collective-permute-start(bf16[64,512]{1,0:T(8,128)(2,1)S(1)} %get-tuple-element.22), channel_id=1, source_target_pairs={{1,0},{2,1},{3,2},{4,3},{5,4},{6,5},{7,6},{9,8},{10,9},{11,10},{12... | collective-permute-start | bytes 196616 | tf_op jit(solution)/shard_map/ppermute | solution.py:25
  57.4 1.9 %collective-permute-start.5 = (bf16[64,512]{1,0:T(8,128)(2,1)S(1)}, bf16[64,512]{1,0:T(8,128)(2,1)S(1)}, u32[]{:S(2)}, u32[]{:S(2)}) collective-permute-start(bf16[64,512]{1,0:T(8,128)(2,1)S(1)} %get-tuple-element.23), channel_id=1, source_target_pairs={{0,8},{8,16},{16,24},{24,32},{32,40},{40,48},{48,56},{56,64},{64,7... | collective-permute-start | bytes 196616 | tf_op jit(solution)/shard_map/ppermute | solution.py:19
  59.3 1.9 %convolution_add_fusion.2 = f32[128,512]{1,0:T(8,128)S(1)} fusion(f32[512,1536]{1,0:T(8,128)} %copy-done, f32[384,512]{1,0:T(8,128)} %get-tuple-element.32, bf16[128,512]{1,0:T(8,128)(2,1)S(1)} %copy-done.9, s32[512]{0:T(512)S(1)} %copy-done.10), kind=kOutput, calls=%fused_computation.14 | convolution fusion | flops 402915328 | bytes 1705984 | tf_op jit(solution)/shard_map/dot_general | solution.py:45
  61.3 42.3 %shard_map.138 = (f32[24,512]{1,0:T(8,128)S(1)}, f32[8,512]{1,0:T(8,128)S(1)}) custom-call(bf16[2,8,8,32,128]{4,3,2,1,0:T(8,128)(2,1)S(1)} %copy.23.grads_a, bf16[2,8,8,32,128]{4,3,2,1,0:T(8,128)(2,1)S(1)} %get-tuple-element.18.grads_b, f32[8,128]{1,0:T(8,128)S(1)} %bitcast.49), custom_call_target="tpu_custom_call" | custom-call | tf_op jit(solution)/shard_map/pallas_call | solution.py:282
  103.7 1.0 copy.24
  104.7 1.0 fusion.3
  105.6 0.6 copy.31
  106.3 0.6 copy.32
  (50 shorter events, 3.6 us)
Async XLA Ops:
  0.6 28.3 %copy-start.4 = (bf16[128,512]{1,0:T(8,128)(2,1)S(1)}, bf16[128,512]{1,0:T(8,128)(2,1)}, u32[]{:S(2)}) copy-start(bf16[128,512]{1,0:T(8,128)(2,1)} %param.11) | copy-start | bytes 393220
  0.6 27.2 %copy-start.6 = (bf16[512,512]{1,0:T(8,128)(2,1)S(1)}, bf16[512,512]{1,0:T(8,128)(2,1)}, u32[]{:S(2)}) copy-start(bf16[512,512]{1,0:T(8,128)(2,1)} %param.16) | copy-start | bytes 1572868
  0.7 27.3 %copy-start.5 = (bf16[512,512]{1,0:T(8,128)(2,1)S(1)}, bf16[512,512]{1,0:T(8,128)(2,1)}, u32[]{:S(2)}) copy-start(bf16[512,512]{1,0:T(8,128)(2,1)} %param.12) | copy-start | bytes 1572868
  0.7 28.3 %copy-start.10 = (s32[512]{0:T(512)S(1)}, s32[512]{0:T(512)}, u32[]{:S(2)}) copy-start(s32[512]{0:T(512)} %param.21) | copy-start | bytes 6148
  2.0 27.4 %collective-permute-start = (bf16[64,512]{1,0:T(8,128)(2,1)S(1)}, bf16[64,512]{1,0:T(8,128)(2,1)S(1)}, u32[]{:S(2)}, u32[]{:S(2)}) collective-permute-start(bf16[64,512]{1,0:T(8,128)(2,1)S(1)} %get-tuple-element.24), channel_id=1, source_target_pairs={{0,8},{8,16},{16,24},{24,32},{32,40},{40,48},{48,56},{56,64},{64,7... | collective-permute-start | bytes 196616 | tf_op jit(solution)/shard_map/ppermute | solution.py:19
  6.0 23.4 %collective-permute-start.3 = (bf16[64,512]{1,0:T(8,128)(2,1)S(1)}, bf16[64,512]{1,0:T(8,128)(2,1)S(1)}, u32[]{:S(2)}, u32[]{:S(2)}) collective-permute-start(bf16[64,512]{1,0:T(8,128)(2,1)S(1)} %get-tuple-element.25), channel_id=1, source_target_pairs={{1,0},{2,1},{3,2},{4,3},{5,4},{6,5},{7,6},{9,8},{10,9},{11,10},{12... | collective-permute-start | bytes 196616 | tf_op jit(solution)/shard_map/ppermute | solution.py:25
  12.7 16.8 %collective-permute-start.2 = (bf16[64,512]{1,0:T(8,128)(2,1)S(1)}, bf16[64,512]{1,0:T(8,128)(2,1)S(1)}, u32[]{:S(2)}, u32[]{:S(2)}) collective-permute-start(bf16[64,512]{1,0:T(8,128)(2,1)S(1)} %get-tuple-element.26), channel_id=1, source_target_pairs={{0,1},{1,2},{2,3},{3,4},{4,5},{5,6},{6,7},{8,9},{9,10},{10,11},{11... | collective-permute-start | bytes 196616 | tf_op jit(solution)/shard_map/ppermute | solution.py:25
  14.6 14.9 %collective-permute-start.1 = (bf16[64,512]{1,0:T(8,128)(2,1)S(1)}, bf16[64,512]{1,0:T(8,128)(2,1)S(1)}, u32[]{:S(2)}, u32[]{:S(2)}) collective-permute-start(bf16[64,512]{1,0:T(8,128)(2,1)S(1)} %get-tuple-element.27), channel_id=1, source_target_pairs={{0,504},{8,0},{16,8},{24,16},{32,24},{40,32},{48,40},{56,48},{64,5... | collective-permute-start | bytes 196616 | tf_op jit(solution)/shard_map/ppermute | solution.py:19
  26.0 3.5 %copy-start.11 = (s32[512]{0:T(512)S(1)}, s32[512]{0:T(512)}, u32[]{:S(2)}) copy-start(s32[512]{0:T(512)} %param.20) | copy-start | bytes 6148
  27.8 2.3 %copy-start.1 = (bf16[1536,512]{1,0:T(8,128)(2,1)S(1)}, bf16[1536,512]{1,0:T(8,128)(2,1)}, u32[]{:S(2)}) copy-start(bf16[1536,512]{1,0:T(8,128)(2,1)} %param.14) | copy-start | bytes 4718596
  29.0 1.2 %copy-start.7 = (bf16[512,512]{0,1:T(8,128)(2,1)S(1)}, bf16[512,512]{0,1:T(8,128)(2,1)}, u32[]{:S(2)}) copy-start(bf16[512,512]{0,1:T(8,128)(2,1)} %copy.19) | copy-start | bytes 1572868
  31.2 0.9 copy-start.8
  37.2 1.9 %copy-start = (f32[512,1536]{1,0:T(8,128)}, f32[512,1536]{1,0:T(8,128)S(1)}, u32[]{:S(2)}) copy-start(f32[512,1536]{1,0:T(8,128)S(1)} %fusion.33) | copy-start | bytes 9437188
  44.0 1.4 %copy-start.2 = (f32[512,512]{1,0:T(8,128)S(1)}, f32[512,512]{1,0:T(8,128)}, u32[]{:S(2)}) copy-start(f32[512,512]{1,0:T(8,128)} %slice.77) | copy-start | bytes 3145732
  46.7 12.6 %copy-start.9 = (bf16[128,512]{1,0:T(8,128)(2,1)S(1)}, bf16[128,512]{1,0:T(8,128)(2,1)}, u32[]{:S(2)}) copy-start(bf16[128,512]{1,0:T(8,128)(2,1)} %param.13) | copy-start | bytes 393220
  46.7 14.5 %copy-start.3 = (bf16[2,8,8,32,128]{4,3,1,2,0:T(8,128)(2,1)S(1)}, bf16[2,8,8,32,128]{4,3,1,2,0:T(8,128)(2,1)}, u32[]{:S(2)}) copy-start(bf16[2,8,8,32,128]{4,3,1,2,0:T(8,128)(2,1)} %get-tuple-element.19) | copy-start | bytes 3145732
  48.2 56.4 %collective-permute-start.4 = (bf16[64,512]{1,0:T(8,128)(2,1)S(1)}, bf16[64,512]{1,0:T(8,128)(2,1)S(1)}, u32[]{:S(2)}, u32[]{:S(2)}) collective-permute-start(bf16[64,512]{1,0:T(8,128)(2,1)S(1)} %get-tuple-element.20), channel_id=1, source_target_pairs={{0,504},{8,0},{16,8},{24,16},{32,24},{40,32},{48,40},{56,48},{64,5... | collective-permute-start | bytes 196616 | tf_op jit(solution)/shard_map/ppermute | solution.py:19
  51.9 52.8 %collective-permute-start.7 = (bf16[64,512]{1,0:T(8,128)(2,1)S(1)}, bf16[64,512]{1,0:T(8,128)(2,1)S(1)}, u32[]{:S(2)}, u32[]{:S(2)}) collective-permute-start(bf16[64,512]{1,0:T(8,128)(2,1)S(1)} %get-tuple-element.21), channel_id=1, source_target_pairs={{0,1},{1,2},{2,3},{3,4},{4,5},{5,6},{6,7},{8,9},{9,10},{10,11},{11... | collective-permute-start | bytes 196616 | tf_op jit(solution)/shard_map/ppermute | solution.py:25
  55.4 49.2 %collective-permute-start.6 = (bf16[64,512]{1,0:T(8,128)(2,1)S(1)}, bf16[64,512]{1,0:T(8,128)(2,1)S(1)}, u32[]{:S(2)}, u32[]{:S(2)}) collective-permute-start(bf16[64,512]{1,0:T(8,128)(2,1)S(1)} %get-tuple-element.22), channel_id=1, source_target_pairs={{1,0},{2,1},{3,2},{4,3},{5,4},{6,5},{7,6},{9,8},{10,9},{11,10},{12... | collective-permute-start | bytes 196616 | tf_op jit(solution)/shard_map/ppermute | solution.py:25
  57.4 47.3 %collective-permute-start.5 = (bf16[64,512]{1,0:T(8,128)(2,1)S(1)}, bf16[64,512]{1,0:T(8,128)(2,1)S(1)}, u32[]{:S(2)}, u32[]{:S(2)}) collective-permute-start(bf16[64,512]{1,0:T(8,128)(2,1)S(1)} %get-tuple-element.23), channel_id=1, source_target_pairs={{0,8},{8,16},{16,24},{24,32},{32,40},{40,48},{48,56},{56,64},{64,7... | collective-permute-start | bytes 196616 | tf_op jit(solution)/shard_map/ppermute | solution.py:19
  61.3 43.4 %copy-start.12 = (s32[1,4,64]{2,1,0:T(4,128)S(1)}, s32[1,4,64]{2,1,0:T(4,128)}, u32[]{:S(2)}) copy-start(s32[1,4,64]{2,1,0:T(4,128)} %param.19) | copy-start | bytes 3076

commit v2 on v0

v2 whole, which is shorter than its diff:
```python
import math

import jax
import jax.numpy as jnp
from jax import lax
from jax.experimental import pallas as pl
from jax.experimental.pallas import tpu as pltpu
from jax.sharding import Mesh
from jax.sharding import PartitionSpec as P

WIDE = ("z", "y")
ALL = ("z", "y", "x", "c")
MESH = pl.DeviceIdType.MESH
F32 = jnp.float32
BF16 = jnp.bfloat16
ROWS = 256


def dot(a, b):
    return jnp.dot(a, b, preferred_element_type=F32)


def dot_nt(a, b):
    return lax.dot_general(a, b, (((1,), (1,)), ((), ())), preferred_element_type=F32)


class Comm:
    def __init__(self, send_sems, recv_sems):
        self.send_sems, self.recv_sems, self.used, self.started = send_sems, recv_sems, 0, []

    def copy(self, src, dst, to):
        copy = pltpu.make_async_remote_copy(
            src_ref=src,
            dst_ref=dst,
            send_sem=self.send_sems.at[self.used],
            recv_sem=self.recv_sems.at[self.used],
            device_id=to,
            device_id_type=MESH,
        )
        self.used += 1
        self.started.append(copy)
        copy.start()
        return copy

    def drain(self):
        for copy in self.started:
            copy.wait_send()


class Ring:
    def __init__(self, comm, axis, own, paired, staged, slots):
        self.comm, self.axis, self.own, self.paired = comm, axis, own, paired
        self.count, self.me = lax.axis_size(axis), lax.axis_index(axis)
        self.half = own.shape[1] // 2
        self.chains = []
        used = 0
        for half in (0, 1):
            for sign in (-1, 1):
                hops = self.count // 2 - (0 if (sign < 0) == (half == 0) else 1)
                span = pl.ds(used, max(hops, 1))
                self.chains.append((half, sign, hops, staged.at[span], slots.at[span]))
                used += hops
        self.last = [None] * 4

    def value(self, owner, half):
        part = pl.ds(half * self.half, self.half)
        return self.own[owner, part] + self.paired[owner, part].astype(F32)

    def step(self, step):
        for i, (half, sign, hops, staged, slots) in enumerate(self.chains):
            if step >= hops:
                continue
            owner = lax.rem(self.me + sign * (hops - step) + self.count, self.count)
            value = self.value(owner, half)
            if step:
                self.last[i].wait_recv()
                value = value + slots[step - 1].astype(F32)
            staged[step] = value.astype(BF16)
            to = lax.rem(self.me + sign + self.count, self.count)
            self.last[i] = self.comm.copy(staged.at[step], slots.at[step], {self.axis: to})

    def finish(self, over, over_sent):
        for half in (0, 1):
            value = self.value(self.me, half)
            for i, (chain_half, _, hops, _, slots) in enumerate(self.chains):
                if chain_half == half and hops:
                    self.last[i].wait_recv()
                    value = value + slots[hops - 1].astype(F32)
            part = pl.ds(half * self.half, self.half)
            over[part] = value
            over_sent[part] = value.astype(BF16)


def offsets(count):
    return sorted(range(1, count), key=lambda k: -min(k, count - k))


def scatter(comm, axis, parts, slots):
    count, me = lax.axis_size(axis), lax.axis_index(axis)
    copies = []
    for k in offsets(count):
        peer = lax.rem(me + k, count)
        copies.append(comm.copy(parts(peer), slots.at[k - 1], {axis: peer}))
    return copies


def total_of(copies, own, slots):
    value = own
    for copy in copies:
        copy.wait_recv()
    for k in range(len(copies)):
        value = value + slots[k].astype(F32)
    return value


def narrow_peers():
    across, cores = lax.axis_size("x"), lax.axis_size("c")
    x, c = lax.axis_index("x"), lax.axis_index("c")
    steps = offsets(across) + [0]
    return [
        {"x": lax.rem(x + i, across), "c": lax.rem(c + j, cores)}
        for i in steps
        for j in range(cores)
        if i or j
    ]


def wide_neighbour(step):
    nz, ny = lax.axis_size("z"), lax.axis_size("y")
    index = lax.rem(lax.axis_index("z") * ny + lax.axis_index("y") + step + nz * ny, nz * ny)
    return {"z": index // ny, "y": lax.rem(index, ny)}


def narrow_neighbour(step):
    across, cores = lax.axis_size("x"), lax.axis_size("c")
    count = across * cores
    index = lax.rem(lax.axis_index("x") * cores + lax.axis_index("c") + step + count, count)
    return {"x": index // cores, "c": lax.rem(index, cores)}


def greeted():
    found = [wide_neighbour(1), wide_neighbour(-1)]
    for axis in ("z", "y"):
        count, me = lax.axis_size(axis), lax.axis_index(axis)
        found += [{axis: lax.rem(me + k, count)} for k in offsets(count)]
    return found + narrow_peers()


def as_columns(row):
    blocks = [
        jnp.transpose(jnp.broadcast_to(row[:, 128 * i : 128 * (i + 1)], (128, 128)))
        for i in range(row.shape[1] // 128)
    ]
    return jnp.concatenate(blocks, 0)


def hot_rows(row, count):
    ids = lax.broadcasted_iota(jnp.int32, (count, row.shape[1]), 0)
    return jnp.where(ids == row, 1.0, 0.0).astype(BF16)


def hot_columns(row, count):
    columns = as_columns(row)
    ids = lax.broadcasted_iota(jnp.int32, columns.shape, 1)
    blocks = [jnp.where(columns == ids + 128 * i, 1.0, 0.0) for i in range(count // 128)]
    return jnp.concatenate(blocks, 1).astype(BF16)


def clip_rows(grad_sq, weight_sq, which):
    ratio = jnp.sqrt((grad_sq + 1e-06) / (weight_sq + 1e-06))
    rows = lax.broadcasted_iota(jnp.int32, ratio.shape, 0)
    mine = lax.rem(rows, 2) == which
    mean_ratio = jnp.sum(jnp.where(mine, ratio, 0.0)) / (ratio.shape[0] // 2 * ratio.shape[1])
    return jnp.minimum(1.0 / (mean_ratio * jnp.sqrt(weight_sq + 1e-06)), 1.0 / jnp.sqrt(grad_sq + 1e-06))


def slab_rows(first, second):
    rows = []
    for i in range(4):
        columns = slice(128 * i, 128 * (i + 1))
        rows += [
            jnp.sum(first[:, columns], 0, keepdims=True),
            jnp.sum(second[:, columns], 0, keepdims=True),
        ]
    return jnp.concatenate(rows, 0)


def split_blocks(value, out_a, out_b, rows):
    ny, nz = out_a.shape[:2]
    height = value.shape[0] // (ny * nz)
    lower = value[:, :128].reshape(nz, ny, height, 128)
    for y in range(ny):
        out_a[y, :, rows, :] = lower[:, y].astype(out_a.dtype)
    out_b[:, :, rows, :] = value[:, 128:].reshape(nz, ny, height, 128).astype(out_b.dtype)


def kernel(
    ids,
    vectors,
    node_hbm,
    edge_hbm,
    cot_hbm,
    w_first_hbm,
    w_second_hbm,
    node_grad_out,
    edge_grad_out,
    first_out,
    second_out,
    table,
    edge,
    cot,
    w_first,
    w_second,
    outgoing,
    inputs_t,
    preact,
    upstream,
    activation_t,
    norm_back,
    pre_back,
    from_sender,
    weight_sq,
    halo_grad,
    returned,
    local_grad,
    sent_a,
    sent_b,
    from_core_a,
    from_core_b,
    own_a,
    own_b,
    staged_a,
    staged_b,
    ring_a,
    ring_b,
    over_a,
    over_b,
    over_sent_a,
    over_sent_b,
    cross_a,
    cross_b,
    share,
    shares,
    squares,
    squares_in,
    load_sems,
    send_sems,
    recv_sems,
):
    comm = Comm(send_sems, recv_sems)
    c = lax.axis_index("c")
    nz, ny, across = lax.axis_size("z"), lax.axis_size("y"), lax.axis_size("x")
    nodes, width = node_hbm.shape
    edges = edge_hbm.shape[0]
    slots = outgoing.shape[1]
    barrier = pltpu.get_barrier_semaphore()
    peers = greeted()
    for peer in peers:
        pl.semaphore_signal(barrier, 1, device_id=peer, device_id_type=MESH)
    loads = [
        pltpu.make_async_copy(src, dst, load_sems.at[i])
        for i, (src, dst) in enumerate(
            (
                (node_hbm, table.at[pl.ds(0, nodes)]),
                (edge_hbm, edge),
                (w_first_hbm, w_first),
                (cot_hbm, cot),
                (w_second_hbm, w_second),
            )
        )
    ]
    for load in loads:
        load.start()
    send_row = ids[:, : 4 * slots]
    sender_row = ids[:, 4 * slots : 4 * slots + edges]
    receiver_row = ids[:, 4 * slots + edges :]
    send_hot = hot_columns(send_row, nodes)
    receiver_hot = hot_columns(receiver_row, nodes)
    loads[0].wait()
    node = table[pl.ds(0, nodes)]
    outgoing[...] = dot(send_hot, node).astype(BF16).reshape(4, slots, width)
    receiver_rows = dot(receiver_hot, node).astype(BF16)
    inputs_t[pl.ds(2 * width, width)] = jnp.transpose(receiver_rows)
    loads[1].wait()
    loads[2].wait()
    preact[...] = (
        dot(edge[...], w_first[pl.ds(0, width)])
        + dot(receiver_rows, w_first[pl.ds(2 * width, width)])
        + vectors[0:1]
    )
    pl.semaphore_wait(barrier, len(peers))
    halo = [
        comm.copy(outgoing.at[k], table.at[pl.ds(nodes + k * slots, slots)], to)
        for k, to in enumerate(
            (wide_neighbour(1), wide_neighbour(-1), narrow_neighbour(1), narrow_neighbour(-1))
        )
    ]
    inputs_t[pl.ds(0, width)] = jnp.transpose(edge[...])
    from_sender[...] = hot_columns(sender_row, table.shape[0])
    loads[3].wait()
    upstream[...] = dot(receiver_hot, cot[...])
    loads[4].wait()
    weight_sq[...] = slab_rows(jnp.square(w_first[...].astype(F32)), jnp.square(w_second[...].astype(F32)))
    for copy in halo:
        copy.wait_recv()
    for i in range(edges // ROWS):
        rows = pl.ds(i * ROWS, ROWS)
        sender_rows = dot(from_sender[rows], table[...]).astype(BF16)
        inputs_t[pl.ds(width, width), rows] = jnp.transpose(sender_rows)
        pre = preact[rows] + dot(sender_rows, w_first[pl.ds(width, width)])
        sigma = 1.0 / (1.0 + jnp.exp(-pre))
        activation = (pre * sigma).astype(BF16)
        activation_t[:, rows] = jnp.transpose(activation)
        slope = sigma * (1.0 + pre * (1.0 - sigma))
        second_pre = dot(activation, w_second[...]) + vectors[1:2]
        centered = second_pre - jnp.mean(second_pre, -1, keepdims=True)
        variance = jnp.mean(centered * centered, -1, keepdims=True)
        inv_std = lax.rsqrt(variance + 1e-05)
        normalized = centered * inv_std
        scaled = upstream[rows] * vectors[2:3]
        back = (
            inv_std
            * (
                scaled
                - jnp.mean(scaled, -1, keepdims=True)
                - normalized * jnp.mean(scaled * normalized, -1, keepdims=True)
            )
        ).astype(BF16)
        norm_back[rows] = back
        pre_back[rows] = (dot_nt(back, w_second[...]) * slope).astype(BF16)

    other = 1 - c
    first_rows, second_rows = pl.ds(0, first_out.shape[0]), pl.ds(first_out.shape[0], second_out.shape[0])
    for half, out_a, out_b in ((other, sent_a, sent_b), (c, own_a, own_b)):
        columns = pl.ds(pl.multiple_of(half * 256, 256), 256)
        split_blocks(dot(activation_t[...], norm_back[:, columns]), out_a, out_b, second_rows)
        split_blocks(dot(inputs_t[...], pre_back[:, columns]), out_a, out_b, first_rows)
        if out_a is sent_a:
            pair = [
                comm.copy(sent_a, from_core_a, {"c": other}),
                comm.copy(sent_b, from_core_b, {"c": other}),
            ]
    for copy in pair:
        copy.wait_recv()
    rings = (
        Ring(comm, "y", own_a, from_core_a, staged_a, ring_a),
        Ring(comm, "z", own_b, from_core_b, staged_b, ring_b),
    )

    def table_part():
        sums = dot(hot_rows(sender_row, table.shape[0]), pre_back[...]).astype(BF16)
        grads = dot_nt(sums, w_first[pl.ds(width, width)])
        local_grad[...] = grads[:nodes]
        halo_grad[...] = grads[nodes:].astype(BF16).reshape(4, slots, width)

    def receiver_part():
        sums = dot(hot_rows(receiver_row, nodes), pre_back[...]).astype(BF16)
        local_grad[...] += dot_nt(sums, w_first[pl.ds(2 * width, width)]) + cot[...].astype(F32)

    def edge_part():
        edge_grad_out[...] = (upstream[...] + dot_nt(pre_back[...], w_first[pl.ds(0, width)])).astype(BF16)

    work = [table_part, receiver_part, edge_part]
    for step in range(max(nz, ny) // 2):
        for ring in rings:
            ring.step(step)
        if work:
            work.pop(0)()
    for rest in work:
        rest()
    rings[0].finish(over_a, over_sent_a)
    to_z = scatter(comm, "z", lambda peer: over_sent_a.at[peer], cross_a)
    rings[1].finish(over_b, over_sent_b)
    to_y = scatter(comm, "y", lambda peer: over_sent_b.at[peer], cross_b)
    share[0] = total_of(to_z, over_a[lax.axis_index("z")], cross_a).astype(BF16)
    share[1] = total_of(to_y, over_b[lax.axis_index("y")], cross_b).astype(BF16)
    here = lax.axis_index("x") * 2 + c
    shares[here] = share[...]
    copies = [comm.copy(share, shares.at[here], device) for device in narrow_peers()]
    for copy in copies:
        copy.wait_recv()
    slabs = []
    for core in (0, 1):
        for i in (0, 1):
            value = shares[core, i].astype(F32)
            for x in range(1, across):
                value = value + shares[2 * x + core, i].astype(F32)
            slabs.append(value)
    cut = first_out.shape[0]
    grads = jnp.concatenate(slabs, 1)
    square = grads * grads
    squares[0] = slab_rows(square[:cut], square[cut:])
    copies = scatter(comm, "y", lambda peer: squares.at[0], squares_in.at[pl.ds(0, ny - 1)])
    halo = [
        comm.copy(halo_grad.at[k], returned.at[k], to)
        for k, to in enumerate(
            (wide_neighbour(-1), wide_neighbour(1), narrow_neighbour(-1), narrow_neighbour(1))
        )
    ]
    squares[1] = total_of(copies, squares[0], squares_in.at[pl.ds(0, ny - 1)])
    copies = scatter(comm, "z", lambda peer: squares.at[1], squares_in.at[pl.ds(ny - 1, nz - 1)])
    for copy in halo:
        copy.wait_recv()
    node_grad_out[...] = (
        local_grad[...] + dot(hot_rows(send_row, nodes), returned[...].reshape(4 * slots, width))
    ).astype(BF16)
    grad_sq = total_of(copies, squares[1], squares_in.at[pl.ds(ny - 1, nz - 1)])
    factors = [clip_rows(grad_sq, weight_sq[...], which) for which in (0, 1)]
    for i in range(4):
        columns = slice(128 * i, 128 * (i + 1))
        first = factors[0][2 * i : 2 * i + 1] * math.sqrt(cut * nz * ny)
        second = factors[1][2 * i + 1 : 2 * i + 2] * math.sqrt(second_out.shape[0] * nz * ny)
        first_out[:, columns] = grads[:cut, columns] * first
        second_out[:, columns] = grads[cut:, columns] * second
    comm.drain()


def per_device(
    node_latent,
    edge_latent,
    node_cotangent,
    w_first,
    bias_first,
    w_second,
    bias_second,
    norm_gain,
    send_map,
    edge_sender,
    edge_receiver,
):
    nz, ny, across = lax.axis_size("z"), lax.axis_size("y"), lax.axis_size("x")
    nodes, width = node_latent.shape
    edges = edge_latent.shape[0]
    slots = send_map.shape[2]
    table_rows = nodes + 4 * slots
    first_rows, second_rows = w_first.shape[0] // (nz * ny), w_second.shape[0] // (nz * ny)
    rows = first_rows + second_rows
    ids = jnp.concatenate([send_map.reshape(4 * slots), edge_sender, edge_receiver]).reshape(1, -1)
    vectors = jnp.stack([bias_first, bias_second, norm_gain]).astype(F32)
    vmem = pl.BlockSpec(memory_space=pltpu.VMEM)
    hbm = pl.BlockSpec(memory_space=pl.ANY)
    ring_copies = 2 * (ny - 1) + 2 * (nz - 1)
    copies = 8 + 2 + ring_copies + (nz - 1 + ny - 1) + 2 * across - 1 + ny - 1 + nz - 1
    return pl.pallas_call(
        kernel,
        out_shape=(
            jax.ShapeDtypeStruct((nodes, width), BF16),
            jax.ShapeDtypeStruct((edges, width), BF16),
            jax.ShapeDtypeStruct((first_rows, width), F32),
            jax.ShapeDtypeStruct((second_rows, width), F32),
        ),
        in_specs=[vmem] * 2 + [hbm] * 5,
        out_specs=(vmem,) * 4,
        scratch_shapes=[
            pltpu.VMEM((table_rows, width), BF16),
            pltpu.VMEM((edges, width), BF16),
            pltpu.VMEM((nodes, width), BF16),
            pltpu.VMEM((3 * width, width), BF16),
            pltpu.VMEM((width, width), BF16),
            pltpu.VMEM((4, slots, width), BF16),
            pltpu.VMEM((3 * width, edges), BF16),
            pltpu.VMEM((edges, width), F32),
            pltpu.VMEM((edges, width), F32),
            pltpu.VMEM((width, edges), BF16),
            pltpu.VMEM((edges, width), BF16),
            pltpu.VMEM((edges, width), BF16),
            pltpu.VMEM((edges, table_rows), BF16),
            pltpu.VMEM((8, 128), F32),
            pltpu.VMEM((4, slots, width), BF16),
            pltpu.VMEM((4, slots, width), BF16),
            pltpu.VMEM((nodes, width), F32),
            pltpu.VMEM((ny, nz, rows, 128), BF16),
            pltpu.VMEM((nz, ny, rows, 128), BF16),
            pltpu.VMEM((ny, nz, rows, 128), BF16),
            pltpu.VMEM((nz, ny, rows, 128), BF16),
            pltpu.VMEM((ny, nz, rows, 128), F32),
            pltpu.VMEM((nz, ny, rows, 128), F32),
            pltpu.VMEM((2 * (ny - 1), nz // 2, rows, 128), BF16),
            pltpu.VMEM((2 * (nz - 1), ny // 2, rows, 128), BF16),
            pltpu.VMEM((2 * (ny - 1), nz // 2, rows, 128), BF16),
            pltpu.VMEM((2 * (nz - 1), ny // 2, rows, 128), BF16),
            pltpu.VMEM((nz, rows, 128), F32),
            pltpu.VMEM((ny, rows, 128), F32),
            pltpu.VMEM((nz, rows, 128), BF16),
            pltpu.VMEM((ny, rows, 128), BF16),
            pltpu.VMEM((nz - 1, rows, 128), BF16),
            pltpu.VMEM((ny - 1, rows, 128), BF16),
            pltpu.VMEM((2, rows, 128), BF16),
            pltpu.VMEM((2 * across, 2, rows, 128), BF16),
            pltpu.VMEM((2, 8, 128), F32),
            pltpu.VMEM((ny - 1 + nz - 1, 8, 128), F32),
            pltpu.SemaphoreType.DMA((5,)),
            pltpu.SemaphoreType.DMA((copies,)),
            pltpu.SemaphoreType.DMA((copies,)),
        ],
        compiler_params=pltpu.CompilerParams(
            collective_id=0, has_side_effects=True, vmem_limit_bytes=56 << 20
        ),
    )(ids, vectors, node_latent, edge_latent, node_cotangent, w_first, w_second)


def solution(mesh):
    finer = Mesh(mesh.devices.reshape(8, 8, 4, 2), ALL)
    in_specs = (
        P(ALL, None),
        P(ALL, None),
        P(ALL, None),
        P(),
        P(),
        P(),
        P(),
        P(),
        P(ALL, None, None),
        P(ALL),
        P(ALL),
    )
    out_specs = (P(ALL, None), P(ALL, None), P(WIDE, None), P(WIDE, None))
    return jax.shard_map(
        per_device, mesh=finer, in_specs=in_specs, out_specs=out_specs, check_vma=False
    )
```

time: 164 us -> 70.8 us (0.43)
  the two profiles are of different devices: /device:TPU:8 before, /device:TPU:1 now
where the time goes in v2:
time: 70.8 us; the launch traced here: 70.4 us
  Pallas kernels  58.8 us (83%)
  local copies, waits for them, and re-layouts  9.58 us (14%)
  other arithmetic  1.32 us (2%)
    pallas_call x1, Pallas kernels, per_device(): pl.pallas_call(kernel, out_shape=(jax.ShapeDtypeStruct((nodes, width), BF...  58.8 us
    unnamed x4, local copies, waits for them, and re-layouts  6.18 us
    another operation x3, local copies, waits for them, and re-layouts, per_device(): vectors = jnp.stack([bias_first, bias_second, norm_gain]).astype(F32)  2.04 us

profile of v2, /device:TPU:1, one launch (start us, length us, event | category | flops | bytes accessed | tf_op | source)
XLA Modules:
  0.0 70.4 jit_solution(8688402148733135992)
XLA Ops:
  0.6 0.8 %reshape.14 = s32[256]{0:T(256)S(1)} reshape(s32[1,4,64]{2,1,0:T(4,128)} %param.19) | data formatting | bytes 2048 | tf_op jit(solution)/shard_map/reshape | solution.py:438
  1.4 0.7 stack.12
  2.1 0.7 stack.13
  2.8 0.7 stack.14
  3.4 0.6 maximum_convert_fusion.vectors
  4.1 0.7 %pad_add_fusion = s32[1280]{0:T(1024)S(1)} fusion(s32[512]{0:T(512)} %param.21, s32[512]{0:T(512)} %param.20, s32[256]{0:T(256)S(1)} %reshape.14), kind=kLoop, calls=%fused_computation | loop fusion | flops 2560 | bytes 10240 | tf_op jit(solution)/shard_map/concatenate | solution.py:438
  4.8 0.6 reshape.15.ids
  5.4 58.8 %shard_map.138 = (bf16[128,512]{1,0:T(8,128)(2,1)}, bf16[512,512]{1,0:T(8,128)(2,1)}, f32[24,512]{1,0:T(8,128)}, f32[8,512]{1,0:T(8,128)}) custom-call(s32[1,1280]{1,0:T(1,128)} %reshape.15.ids, f32[3,512]{1,0:T(4,128)} %maximum_convert_fusion.vectors, bf16[128,512]{1,0:T(8,128)(2,1)} %node_hbm.1, bf16[512,512]{1,0:T(8,128)(2,1)} %edge_hbm.1, ...), custom_call_target="tpu_custom_call" | custom-call | tf_op jit(solution)/shard_map/pallas_call | solution.py:444
  64.2 1.6 %copy.19 = bf16[128,512]{1,0:T(8,128)(2,1)} copy(bf16[128,512]{1,0:T(8,128)(2,1)} %get-tuple-element.8) | data formatting | bytes 262144
  65.8 1.9 %copy.20 = bf16[512,512]{1,0:T(8,128)(2,1)} copy(bf16[512,512]{1,0:T(8,128)(2,1)} %get-tuple-element.9) | data formatting | bytes 1048576
  67.6 1.4 %copy.21 = f32[24,512]{1,0:T(8,128)} copy(f32[24,512]{1,0:T(8,128)} %get-tuple-element.10) | data formatting | bytes 98304
  69.1 1.3 %copy.22 = f32[8,512]{1,0:T(8,128)} copy(f32[8,512]{1,0:T(8,128)} %get-tuple-element.11) | data formatting | bytes 32768

commit v3 on v2

--- a/solution.py
+++ b/solution.py
@@ -26,30 +26,40 @@
 
 class Comm:
     def __init__(self, send_sems, recv_sems):
-        self.send_sems, self.recv_sems, self.used, self.started = send_sems, recv_sems, 0, []
-
-    def copy(self, src, dst, to):
+        self.send_sems, self.recv_sems, self.groups, self.used = send_sems, recv_sems, [], 0
+
+    def group(self, sent):
+        self.groups.append(sent)
+        return len(self.groups) - 1
+
+    def recv_sem(self):
+        self.used += 1
+        return self.recv_sems.at[self.used - 1]
+
+    def copy(self, group, src, dst, to, recv_sem=None):
         copy = pltpu.make_async_remote_copy(
             src_ref=src,
             dst_ref=dst,
-            send_sem=self.send_sems.at[self.used],
-            recv_sem=self.recv_sems.at[self.used],
+            send_sem=self.send_sems.at[group],
+            recv_sem=self.recv_sem() if recv_sem is None else recv_sem,
             device_id=to,
             device_id_type=MESH,
         )
-        self.used += 1
-        self.started.append(copy)
         copy.start()
         return copy
 
     def drain(self):
-        for copy in self.started:
-            copy.wait_send()
+        for i, sent in enumerate(self.groups):
+            wait_for(sent, self.send_sems.at[i])
+
+
+def wait_for(ref, sem):
+    pltpu.make_async_copy(ref, ref, sem).wait()
 
 
 class Ring:
-    def __init__(self, comm, axis, own, paired, staged, slots):
-        self.comm, self.axis, self.own, self.paired = comm, axis, own, paired
+    def __init__(self, comm, axis, sent, paired, own, staged, slots):
+        self.comm, self.axis, self.sent, self.paired, self.own = comm, axis, sent, paired, own
         self.count, self.me = lax.axis_size(axis), lax.axis_index(axis)
         self.half = own.shape[1] // 2
         self.chains = []
@@ -61,27 +71,45 @@
                 self.chains.append((half, sign, hops, staged.at[span], slots.at[span]))
                 used += hops
         self.last = [None] * 4
-
-    def value(self, owner, half):
+        self.staged = staged
+        self.pairs = {}
+        self.pair_group = comm.group(sent)
+
+    def at(self, offset):
+        return lax.rem(self.me + offset + self.count, self.count)
+
+    def pair(self, offset, other):
+        owner = self.at(offset)
+        self.pairs[offset % self.count] = self.comm.copy(
+            self.pair_group, self.sent.at[owner], self.paired.at[owner], {"c": other}
+        )
+
+    def value(self, offset, half):
+        pair = self.pairs.pop(offset % self.count, None)
+        if pair is not None:
+            pair.wait_recv()
+        owner = self.at(offset)
         part = pl.ds(half * self.half, self.half)
         return self.own[owner, part] + self.paired[owner, part].astype(F32)
 
     def step(self, step):
+        if step == 0:
+            self.group = self.comm.group(self.staged)
         for i, (half, sign, hops, staged, slots) in enumerate(self.chains):
             if step >= hops:
                 continue
-            owner = lax.rem(self.me + sign * (hops - step) + self.count, self.count)
-            value = self.value(owner, half)
+            value = self.value(sign * (hops - step), half)
             if step:
                 self.last[i].wait_recv()
                 value = value + slots[step - 1].astype(F32)
             staged[step] = value.astype(BF16)
-            to = lax.rem(self.me + sign + self.count, self.count)
-            self.last[i] = self.comm.copy(staged.at[step], slots.at[step], {self.axis: to})
+            self.last[i] = self.comm.copy(
+                self.group, staged.at[step], slots.at[step], {self.axis: self.at(sign)}
+            )
 
     def finish(self, over, over_sent):
         for half in (0, 1):
-            value = self.value(self.me, half)
+            value = self.value(0, half)
             for i, (chain_half, _, hops, _, slots) in enumerate(self.chains):
                 if chain_half == half and hops:
                     self.last[i].wait_recv()
@@ -97,18 +125,18 @@
 
 def scatter(comm, axis, parts, slots):
     count, me = lax.axis_size(axis), lax.axis_index(axis)
-    copies = []
+    sem, group = comm.recv_sem(), comm.group(slots)
     for k in offsets(count):
         peer = lax.rem(me + k, count)
-        copies.append(comm.copy(parts(peer), slots.at[k - 1], {axis: peer}))
-    return copies
-
-
-def total_of(copies, own, slots):
+        comm.copy(group, parts(peer), slots.at[k - 1], {axis: peer}, sem)
+    return slots, sem
+
+
+def total_of(arriving, own):
+    slots, sem = arriving
+    wait_for(slots, sem)
     value = own
-    for copy in copies:
-        copy.wait_recv()
-    for k in range(len(copies)):
+    for k in range(slots.shape[0]):
         value = value + slots[k].astype(F32)
     return value
 
@@ -195,17 +223,27 @@
 
 
 def kernel(
-    ids,
-    vectors,
+    send_hbm,
+    sender_hbm,
+    receiver_hbm,
+    bias_first_hbm,
+    bias_second_hbm,
+    gain_hbm,
     node_hbm,
     edge_hbm,
     cot_hbm,
     w_first_hbm,
     w_second_hbm,
-    node_grad_out,
-    edge_grad_out,
-    first_out,
-    second_out,
+    node_grad_hbm,
+    edge_grad_hbm,
+    first_hbm,
+    second_hbm,
+    send_map,
+    sender_ids,
+    receiver_ids,
+    bias_first,
+    bias_second,
+    norm_gain,
     table,
     edge,
     cot,
@@ -243,7 +281,12 @@
     shares,
     squares,
     squares_in,
+    node_grad_out,
+    edge_grad_out,
+    first_out,
+    second_out,
     load_sems,
+    store_sems,
     send_sems,
     recv_sems,
 ):
@@ -261,48 +304,54 @@
         pltpu.make_async_copy(src, dst, load_sems.at[i])
         for i, (src, dst) in enumerate(
             (
+                (send_hbm, send_map),
                 (node_hbm, table.at[pl.ds(0, nodes)]),
+                (receiver_hbm, receiver_ids),
                 (edge_hbm, edge),
                 (w_first_hbm, w_first),
+                (bias_first_hbm, bias_first),
+                (sender_hbm, sender_ids),
                 (cot_hbm, cot),
                 (w_second_hbm, w_second),
+                (bias_second_hbm, bias_second),
+                (gain_hbm, norm_gain),
             )
         )
     ]
     for load in loads:
         load.start()
-    send_row = ids[:, : 4 * slots]
-    sender_row = ids[:, 4 * slots : 4 * slots + edges]
-    receiver_row = ids[:, 4 * slots + edges :]
+    loads[0].wait()
+    send_row = jnp.concatenate([send_map[0, k : k + 1, :] for k in range(4)], 1)
     send_hot = hot_columns(send_row, nodes)
-    receiver_hot = hot_columns(receiver_row, nodes)
-    loads[0].wait()
+    loads[1].wait()
     node = table[pl.ds(0, nodes)]
     outgoing[...] = dot(send_hot, node).astype(BF16).reshape(4, slots, width)
+    pl.semaphore_wait(barrier, len(peers))
+    halo_sem, halo_group = comm.recv_sem(), comm.group(outgoing)
+    arriving = table.at[pl.ds(nodes, 4 * slots)]
+    for k, to in enumerate(
+        (wide_neighbour(1), wide_neighbour(-1), narrow_neighbour(1), narrow_neighbour(-1))
+    ):
+        comm.copy(halo_group, outgoing.at[k], table.at[pl.ds(nodes + k * slots, slots)], to, halo_sem)
+    loads[2].wait()
+    receiver_row = receiver_ids[...].reshape(1, edges)
+    receiver_hot = hot_columns(receiver_row, nodes)
     receiver_rows = dot(receiver_hot, node).astype(BF16)
     inputs_t[pl.ds(2 * width, width)] = jnp.transpose(receiver_rows)
-    loads[1].wait()
-    loads[2].wait()
+    for load in loads[3:]:
+        load.wait()
+    vectors = [v[...].astype(F32).reshape(1, width) for v in (bias_first, bias_second, norm_gain)]
     preact[...] = (
         dot(edge[...], w_first[pl.ds(0, width)])
         + dot(receiver_rows, w_first[pl.ds(2 * width, width)])
-        + vectors[0:1]
+        + vectors[0]
     )
-    pl.semaphore_wait(barrier, len(peers))
-    halo = [
-        comm.copy(outgoing.at[k], table.at[pl.ds(nodes + k * slots, slots)], to)
-        for k, to in enumerate(
-            (wide_neighbour(1), wide_neighbour(-1), narrow_neighbour(1), narrow_neighbour(-1))
-        )
-    ]
+    sender_row = sender_ids[...].reshape(1, edges)
     inputs_t[pl.ds(0, width)] = jnp.transpose(edge[...])
     from_sender[...] = hot_columns(sender_row, table.shape[0])
-    loads[3].wait()
     upstream[...] = dot(receiver_hot, cot[...])
-    loads[4].wait()
     weight_sq[...] = slab_rows(jnp.square(w_first[...].astype(F32)), jnp.square(w_second[...].astype(F32)))
-    for copy in halo:
-        copy.wait_recv()
+    wait_for(arriving, halo_sem)
     for i in range(edges // ROWS):
         rows = pl.ds(i * ROWS, ROWS)
         sender_rows = dot(from_sender[rows], table[...]).astype(BF16)
@@ -312,12 +361,12 @@
         activation = (pre * sigma).astype(BF16)
         activation_t[:, rows] = jnp.transpose(activation)
         slope = sigma * (1.0 + pre * (1.0 - sigma))
-        second_pre = dot(activation, w_second[...]) + vectors[1:2]
+        second_pre = dot(activation, w_second[...]) + vectors[1]
         centered = second_pre - jnp.mean(second_pre, -1, keepdims=True)
         variance = jnp.mean(centered * centered, -1, keepdims=True)
         inv_std = lax.rsqrt(variance + 1e-05)
         normalized = centered * inv_std
-        scaled = upstream[rows] * vectors[2:3]
+        scaled = upstream[rows] * vectors[2]
         back = (
             inv_std
             * (
@@ -330,22 +379,21 @@
         pre_back[rows] = (dot_nt(back, w_second[...]) * slope).astype(BF16)
 
     other = 1 - c
-    first_rows, second_rows = pl.ds(0, first_out.shape[0]), pl.ds(first_out.shape[0], second_out.shape[0])
+    rings = (
+        Ring(comm, "y", sent_a, from_core_a, own_a, staged_a, ring_a),
+        Ring(comm, "z", sent_b, from_core_b, own_b, staged_b, ring_b),
+    )
+    cut, rest = first_out.shape[0], second_out.shape[0]
     for half, out_a, out_b in ((other, sent_a, sent_b), (c, own_a, own_b)):
         columns = pl.ds(pl.multiple_of(half * 256, 256), 256)
-        split_blocks(dot(activation_t[...], norm_back[:, columns]), out_a, out_b, second_rows)
-        split_blocks(dot(inputs_t[...], pre_back[:, columns]), out_a, out_b, first_rows)
+        split_blocks(dot(activation_t[...], norm_back[:, columns]), out_a, out_b, pl.ds(cut, rest))
+        split_blocks(dot(inputs_t[...], pre_back[:, columns]), out_a, out_b, pl.ds(0, cut))
         if out_a is sent_a:
-            pair = [
-                comm.copy(sent_a, from_core_a, {"c": other}),
-                comm.copy(sent_b, from_core_b, {"c": other}),
-            ]
-    for copy in pair:
-        copy.wait_recv()
-    rings = (
-        Ring(comm, "y", own_a, from_core_a, staged_a, ring_a),
-        Ring(comm, "z", own_b, from_core_b, staged_b, ring_b),
-    )
+            for i in range(max(ny, nz)):
+                for ring in rings:
+                    order = offsets(ring.count) + [0]
+                    if i < ring.count:
+                        ring.pair(order[i], other)
 
     def table_part():
         sums = dot(hot_rows(sender_row, table.shape[0]), pre_back[...]).astype(BF16)
@@ -357,8 +405,16 @@
         sums = dot(hot_rows(receiver_row, nodes), pre_back[...]).astype(BF16)
         local_grad[...] += dot_nt(sums, w_first[pl.ds(2 * width, width)]) + cot[...].astype(F32)
 
+    stores = []
+
+    def store(src, dst):
+        copy = pltpu.make_async_copy(src, dst, store_sems.at[len(stores)])
+        copy.start()
+        stores.append(copy)
+
     def edge_part():
         edge_grad_out[...] = (upstream[...] + dot_nt(pre_back[...], w_first[pl.ds(0, width)])).astype(BF16)
+        store(edge_grad_out, edge_grad_hbm)
 
     work = [table_part, receiver_part, edge_part]
     for step in range(max(nz, ny) // 2):
@@ -366,17 +422,18 @@
             ring.step(step)
         if work:
             work.pop(0)()
-    for rest in work:
-        rest()
+    for part in work:
+        part()
     rings[0].finish(over_a, over_sent_a)
     to_z = scatter(comm, "z", lambda peer: over_sent_a.at[peer], cross_a)
     rings[1].finish(over_b, over_sent_b)
     to_y = scatter(comm, "y", lambda peer: over_sent_b.at[peer], cross_b)
-    share[0] = total_of(to_z, over_a[lax.axis_index("z")], cross_a).astype(BF16)
-    share[1] = total_of(to_y, over_b[lax.axis_index("y")], cross_b).astype(BF16)
+    share[0] = total_of(to_z, over_a[lax.axis_index("z")]).astype(BF16)
+    share[1] = total_of(to_y, over_b[lax.axis_index("y")]).astype(BF16)
     here = lax.axis_index("x") * 2 + c
     shares[here] = share[...]
-    copies = [comm.copy(share, shares.at[here], device) for device in narrow_peers()]
+    group = comm.group(shares.at[pl.ds(0, 2 * across - 1)])
+    copies = [comm.copy(group, share, shares.at[here], device) for device in narrow_peers()]
     for copy in copies:
         copy.wait_recv()
     slabs = []
@@ -386,33 +443,46 @@
             for x in range(1, across):
                 value = value + shares[2 * x + core, i].astype(F32)
             slabs.append(value)
-    cut = first_out.shape[0]
     grads = jnp.concatenate(slabs, 1)
     square = grads * grads
     squares[0] = slab_rows(square[:cut], square[cut:])
-    copies = scatter(comm, "y", lambda peer: squares.at[0], squares_in.at[pl.ds(0, ny - 1)])
-    halo = [
-        comm.copy(halo_grad.at[k], returned.at[k], to)
-        for k, to in enumerate(
-            (wide_neighbour(-1), wide_neighbour(1), narrow_neighbour(-1), narrow_neighbour(1))
-        )
-    ]
-    squares[1] = total_of(copies, squares[0], squares_in.at[pl.ds(0, ny - 1)])
-    copies = scatter(comm, "z", lambda peer: squares.at[1], squares_in.at[pl.ds(ny - 1, nz - 1)])
-    for copy in halo:
-        copy.wait_recv()
+    to_y = scatter(comm, "y", lambda peer: squares.at[0], squares_in.at[pl.ds(0, ny - 1)])
+    back_sem, back_group = comm.recv_sem(), comm.group(halo_grad)
+    for k, to in enumerate(
+        (wide_neighbour(-1), wide_neighbour(1), narrow_neighbour(-1), narrow_neighbour(1))
+    ):
+        comm.copy(back_group, halo_grad.at[k], returned.at[k], to, back_sem)
+    squares[1] = total_of(to_y, squares[0])
+    to_z = scatter(comm, "z", lambda peer: squares.at[1], squares_in.at[pl.ds(ny - 1, nz - 1)])
+    wait_for(returned, back_sem)
     node_grad_out[...] = (
         local_grad[...] + dot(hot_rows(send_row, nodes), returned[...].reshape(4 * slots, width))
     ).astype(BF16)
-    grad_sq = total_of(copies, squares[1], squares_in.at[pl.ds(ny - 1, nz - 1)])
+    store(node_grad_out, node_grad_hbm)
+    grad_sq = total_of(to_z, squares[1])
     factors = [clip_rows(grad_sq, weight_sq[...], which) for which in (0, 1)]
     for i in range(4):
         columns = slice(128 * i, 128 * (i + 1))
         first = factors[0][2 * i : 2 * i + 1] * math.sqrt(cut * nz * ny)
-        second = factors[1][2 * i + 1 : 2 * i + 2] * math.sqrt(second_out.shape[0] * nz * ny)
+        second = factors[1][2 * i + 1 : 2 * i + 2] * math.sqrt(rest * nz * ny)
         first_out[:, columns] = grads[:cut, columns] * first
         second_out[:, columns] = grads[cut:, columns] * second
+    store(first_out, first_hbm)
+    store(second_out, second_hbm)
     comm.drain()
+    for copy in stores:
+        copy.wait()
+
+
+def deliver(*refs):
+    count = len(refs) // 2
+    copies = [
+        pltpu.make_async_copy(refs[i], refs[count + i], refs[-1].at[i]) for i in range(count)
+    ]
+    for copy in copies:
+        copy.start()
+    for copy in copies:
+        copy.wait()
 
 
 def per_device(
@@ -435,13 +505,10 @@
     table_rows = nodes + 4 * slots
     first_rows, second_rows = w_first.shape[0] // (nz * ny), w_second.shape[0] // (nz * ny)
     rows = first_rows + second_rows
-    ids = jnp.concatenate([send_map.reshape(4 * slots), edge_sender, edge_receiver]).reshape(1, -1)
-    vectors = jnp.stack([bias_first, bias_second, norm_gain]).astype(F32)
     vmem = pl.BlockSpec(memory_space=pltpu.VMEM)
-    hbm = pl.BlockSpec(memory_space=pl.ANY)
-    ring_copies = 2 * (ny - 1) + 2 * (nz - 1)
-    copies = 8 + 2 + ring_copies + (nz - 1 + ny - 1) + 2 * across - 1 + ny - 1 + nz - 1
-    return pl.pallas_call(
+    hbm = pl.BlockSpec(memory_space=pltpu.HBM)
+    copies = 1 + 3 * (ny + nz) - 4 + 2 + 2 * across - 1 + 3
+    results = pl.pallas_call(
         kernel,
         out_shape=(
             jax.ShapeDtypeStruct((nodes, width), BF16),
@@ -449,9 +516,15 @@
             jax.ShapeDtypeStruct((first_rows, width), F32),
             jax.ShapeDtypeStruct((second_rows, width), F32),
         ),
-        in_specs=[vmem] * 2 + [hbm] * 5,
-        out_specs=(vmem,) * 4,
+        in_specs=[hbm] * 11,
+        out_specs=(hbm,) * 4,
         scratch_shapes=[
+            pltpu.VMEM(send_map.shape, jnp.int32),
+            pltpu.VMEM((edges,), jnp.int32),
+            pltpu.VMEM((edges,), jnp.int32),
+            pltpu.VMEM((width,), BF16),
+            pltpu.VMEM((width,), BF16),
+            pltpu.VMEM((width,), BF16),
             pltpu.VMEM((table_rows, width), BF16),
             pltpu.VMEM((edges, width), BF16),
             pltpu.VMEM((nodes, width), BF16),
@@ -489,14 +562,39 @@
             pltpu.VMEM((2 * across, 2, rows, 128), BF16),
             pltpu.VMEM((2, 8, 128), F32),
             pltpu.VMEM((ny - 1 + nz - 1, 8, 128), F32),
-            pltpu.SemaphoreType.DMA((5,)),
-            pltpu.SemaphoreType.DMA((copies,)),
+            pltpu.VMEM((nodes, width), BF16),
+            pltpu.VMEM((edges, width), BF16),
+            pltpu.VMEM((first_rows, width), F32),
+            pltpu.VMEM((second_rows, width), F32),
+            pltpu.SemaphoreType.DMA((11,)),
+            pltpu.SemaphoreType.DMA((4,)),
+            pltpu.SemaphoreType.DMA((11,)),
             pltpu.SemaphoreType.DMA((copies,)),
         ],
         compiler_params=pltpu.CompilerParams(
             collective_id=0, has_side_effects=True, vmem_limit_bytes=56 << 20
         ),
-    )(ids, vectors, node_latent, edge_latent, node_cotangent, w_first, w_second)
+    )(
+        send_map,
+        edge_sender,
+        edge_receiver,
+        bias_first,
+        bias_second,
+        norm_gain,
+        node_latent,
+        edge_latent,
+        node_cotangent,
+        w_first,
+        w_second,
+    )
+    return pl.pallas_call(
+        deliver,
+        out_shape=[jax.ShapeDtypeStruct(v.shape, v.dtype) for v in results],
+        in_specs=[vmem] * 4,
+        out_specs=[hbm] * 4,
+        scratch_shapes=[pltpu.SemaphoreType.DMA((4,))],
+        compiler_params=pltpu.CompilerParams(vmem_limit_bytes=8 << 20),
+    )(*results)
 
 
 def solution(mesh):

time: 70.8 us -> 62.2 us (0.88)
  local copies, waits for them, and re-layouts: 9.58 us -> 3.45 us
  other arithmetic: 1.32 us -> 0 us
  Pallas kernels: 58.8 us -> 57.8 us
    unnamed x4 -> x8, local copies, waits for them, and re-layouts: 6.18 us -> 3.45 us
    another operation x3 -> x0, local copies, waits for them, and re-layouts: 2.04 us -> none  [per_device(): vectors = jnp.stack([bias_first, bias_second, norm_gain]).astype(F32)]
    pallas_call x1, Pallas kernels: 58.8 us -> 56.9 us  [per_device(): pl.pallas_call(kernel, out_shape=(jax.ShapeDtypeStruct((nodes, width), BF...]
    reshape x2 -> x0, local copies, waits for them, and re-layouts: 1.36 us -> none  [the longest x1 0.76 us: per_device(): send_map.reshape(4 * slots)]
    pallas_call x0 -> x1, Pallas kernels: none -> 0.87 us  [per_device(): pl.pallas_call(deliver, out_shape=[jax.ShapeDtypeStruct(v.shape, v.dtype)...]
where the time goes in v3:
time: 62.2 us; the launch traced here: 61.9 us
  Pallas kernels  57.8 us (93%)
  local copies, waits for them, and re-layouts  3.45 us (6%)
  between operations  0.66 us (1%)
    pallas_call x1, Pallas kernels, per_device(): pl.pallas_call(kernel, out_shape=(jax.ShapeDtypeStruct((nodes, width), BF...  56.9 us
    unnamed x8, local copies, waits for them, and re-layouts  3.45 us

profile of v3, /device:TPU:1, one launch (start us, length us, event | category | flops | bytes accessed | tf_op | source)
XLA Modules:
  0.0 61.9 jit_solution(4505087330849860225)
XLA Ops:
  0.6 56.9 %shard_map.138 = (bf16[128,512]{1,0:T(8,128)(2,1)}, bf16[512,512]{1,0:T(8,128)(2,1)}, f32[24,512]{1,0:T(8,128)}, f32[8,512]{1,0:T(8,128)}) custom-call(s32[1,4,64]{2,1,0:T(4,128)} %send_hbm.1, s32[512]{0:T(512)} %sender_hbm.1, s32[512]{0:T(512)} %receiver_hbm.1, bf16[512]{0:T(512)(128)(2,1)} %bias_first_hbm.1, bf16[512]{0:T(512)(128)(2,1)} %bias_second_hbm.1, ...), custom_call_target="tpu_custom_call" | custom-call | tf_op jit(solution)/shard_map/pallas_call | solution.py:511
  57.6 0.0 copy-start
  57.6 1.0 %copy-done = bf16[512,512]{1,0:T(8,128)(2,1)S(1)} copy-done((bf16[512,512]{1,0:T(8,128)(2,1)S(1)}, bf16[512,512]{1,0:T(8,128)(2,1)}, u32[]{:S(2)}) %copy-start) | copy-done | bytes 524312
  58.6 0.0 copy-start.1
  58.6 0.9 %copy-done.1 = bf16[128,512]{1,0:T(8,128)(2,1)S(1)} copy-done((bf16[128,512]{1,0:T(8,128)(2,1)S(1)}, bf16[128,512]{1,0:T(8,128)(2,1)}, u32[]{:S(2)}) %copy-start.1) | copy-done | bytes 131096
  59.5 0.0 copy-start.2
  59.5 0.8 %copy-done.2 = f32[24,512]{1,0:T(8,128)S(1)} copy-done((f32[24,512]{1,0:T(8,128)S(1)}, f32[24,512]{1,0:T(8,128)}, u32[]{:S(2)}) %copy-start.2) | copy-done | bytes 49176
  60.3 0.0 copy-start.3
  60.3 0.7 %copy-done.3 = f32[8,512]{1,0:T(8,128)S(1)} copy-done((f32[8,512]{1,0:T(8,128)S(1)}, f32[8,512]{1,0:T(8,128)}, u32[]{:S(2)}) %copy-start.3) | copy-done | bytes 16408
  61.0 0.9 %shard_map.139 = (bf16[128,512]{1,0:T(8,128)(2,1)}, bf16[512,512]{1,0:T(8,128)(2,1)}, f32[24,512]{1,0:T(8,128)}, f32[8,512]{1,0:T(8,128)}) custom-call(bf16[128,512]{1,0:T(8,128)(2,1)S(1)} %copy-done.1, bf16[512,512]{1,0:T(8,128)(2,1)S(1)} %copy-done, f32[24,512]{1,0:T(8,128)S(1)} %copy-done.2, f32[8,512]{1,0:T(8,128)S(1)} %copy-done.3), custom_call_target="tpu_custom_call" | custom-call | tf_op jit(solution)/shard_map/pallas_call | solution.py:590
Async XLA Ops:
  57.6 1.0 %copy-start = (bf16[512,512]{1,0:T(8,128)(2,1)S(1)}, bf16[512,512]{1,0:T(8,128)(2,1)}, u32[]{:S(2)}) copy-start(bf16[512,512]{1,0:T(8,128)(2,1)} %get-tuple-element.9.refs_1_) | copy-start | bytes 1572868
  58.6 0.9 %copy-start.1 = (bf16[128,512]{1,0:T(8,128)(2,1)S(1)}, bf16[128,512]{1,0:T(8,128)(2,1)}, u32[]{:S(2)}) copy-start(bf16[128,512]{1,0:T(8,128)(2,1)} %get-tuple-element.8.refs_0_) | copy-start | bytes 393220
  59.5 0.8 %copy-start.2 = (f32[24,512]{1,0:T(8,128)S(1)}, f32[24,512]{1,0:T(8,128)}, u32[]{:S(2)}) copy-start(f32[24,512]{1,0:T(8,128)} %get-tuple-element.10.refs_2_) | copy-start | bytes 147460
  60.3 0.7 %copy-start.3 = (f32[8,512]{1,0:T(8,128)S(1)}, f32[8,512]{1,0:T(8,128)}, u32[]{:S(2)}) copy-start(f32[8,512]{1,0:T(8,128)} %get-tuple-element.11.refs_3_) | copy-start | bytes 49156

commit v4 on v3

--- a/solution.py
+++ b/solution.py
@@ -170,7 +170,7 @@
     found = [wide_neighbour(1), wide_neighbour(-1)]
     for axis in ("z", "y"):
         count, me = lax.axis_size(axis), lax.axis_index(axis)
-        found += [{axis: lax.rem(me + k, count)} for k in offsets(count)]
+        found += [{axis: lax.rem(me + k, count)} for k in sorted({1, count - 1})]
     return found + narrow_peers()
 
 
@@ -425,8 +425,8 @@
     for part in work:
         part()
     rings[0].finish(over_a, over_sent_a)
+    rings[1].finish(over_b, over_sent_b)
     to_z = scatter(comm, "z", lambda peer: over_sent_a.at[peer], cross_a)
-    rings[1].finish(over_b, over_sent_b)
     to_y = scatter(comm, "y", lambda peer: over_sent_b.at[peer], cross_b)
     share[0] = total_of(to_z, over_a[lax.axis_index("z")]).astype(BF16)
     share[1] = total_of(to_y, over_b[lax.axis_index("y")]).astype(BF16)
@@ -475,14 +475,18 @@
 
 
 def deliver(*refs):
-    count = len(refs) // 2
-    copies = [
-        pltpu.make_async_copy(refs[i], refs[count + i], refs[-1].at[i]) for i in range(count)
-    ]
-    for copy in copies:
-        copy.start()
-    for copy in copies:
-        copy.wait()
+    count = (len(refs) - 2) // 3
+    sources, targets, held = refs[:count], refs[count : 2 * count], refs[2 * count : 3 * count]
+    moves = []
+    for i in range(count):
+        load = pltpu.make_async_copy(sources[i], held[i], refs[-2].at[i])
+        load.start()
+        moves.append((load, pltpu.make_async_copy(held[i], targets[i], refs[-1].at[i])))
+    for load, store in moves:
+        load.wait()
+        store.start()
+    for _, store in moves:
+        store.wait()
 
 
 def per_device(
@@ -505,7 +509,6 @@
     table_rows = nodes + 4 * slots
     first_rows, second_rows = w_first.shape[0] // (nz * ny), w_second.shape[0] // (nz * ny)
     rows = first_rows + second_rows
-    vmem = pl.BlockSpec(memory_space=pltpu.VMEM)
     hbm = pl.BlockSpec(memory_space=pltpu.HBM)
     copies = 1 + 3 * (ny + nz) - 4 + 2 + 2 * across - 1 + 3
     results = pl.pallas_call(
@@ -590,10 +593,11 @@
     return pl.pallas_call(
         deliver,
         out_shape=[jax.ShapeDtypeStruct(v.shape, v.dtype) for v in results],
-        in_specs=[vmem] * 4,
+        in_specs=[hbm] * 4,
         out_specs=[hbm] * 4,
-        scratch_shapes=[pltpu.SemaphoreType.DMA((4,))],
-        compiler_params=pltpu.CompilerParams(vmem_limit_bytes=8 << 20),
+        scratch_shapes=[pltpu.VMEM(v.shape, v.dtype) for v in results]
+        + [pltpu.SemaphoreType.DMA((4,))] * 2,
+        compiler_params=pltpu.CompilerParams(vmem_limit_bytes=56 << 20),
     )(*results)
 
 

time: 62.2 us -> 58.5 us (0.941)
  local copies, waits for them, and re-layouts: 3.45 us -> 0 us
    unnamed x8 -> x0, local copies, waits for them, and re-layouts: 3.45 us -> none
    pallas_call x1, Pallas kernels: 56.9 us -> 55.7 us  [per_device(): pl.pallas_call(kernel, out_shape=(jax.ShapeDtypeStruct((nodes, width), BF...]
    pallas_call x1, Pallas kernels: 0.87 us -> 1.98 us  [per_device(): pl.pallas_call(deliver, out_shape=[jax.ShapeDtypeStruct(v.shape, v.dtype)...]
where the time goes in v4:
time: 58.5 us; the launch traced here: 58.3 us
  Pallas kernels  57.6 us (98%)
  between operations  0.64 us (1%)
    pallas_call x1, Pallas kernels, per_device(): pl.pallas_call(kernel, out_shape=(jax.ShapeDtypeStruct((nodes, width), BF...  55.7 us
    pallas_call x1, Pallas kernels, per_device(): pl.pallas_call(deliver, out_shape=[jax.ShapeDtypeStruct(v.shape, v.dtype)...  1.98 us

profile of v4, /device:TPU:1, one launch (start us, length us, event | category | flops | bytes accessed | tf_op | source)
XLA Modules:
  0.0 58.3 jit_solution(2135907815423902650)
XLA Ops:
  0.6 55.7 %shard_map.138 = (bf16[128,512]{1,0:T(8,128)(2,1)}, bf16[512,512]{1,0:T(8,128)(2,1)}, f32[24,512]{1,0:T(8,128)}, f32[8,512]{1,0:T(8,128)}) custom-call(s32[1,4,64]{2,1,0:T(4,128)} %send_hbm.1, s32[512]{0:T(512)} %sender_hbm.1, s32[512]{0:T(512)} %receiver_hbm.1, bf16[512]{0:T(512)(128)(2,1)} %bias_first_hbm.1, bf16[512]{0:T(512)(128)(2,1)} %bias_second_hbm.1, ...), custom_call_target="tpu_custom_call" | custom-call | tf_op jit(solution)/shard_map/pallas_call | solution.py:514
  56.3 2.0 %shard_map.139 = (bf16[128,512]{1,0:T(8,128)(2,1)}, bf16[512,512]{1,0:T(8,128)(2,1)}, f32[24,512]{1,0:T(8,128)}, f32[8,512]{1,0:T(8,128)}) custom-call(bf16[128,512]{1,0:T(8,128)(2,1)} %get-tuple-element.8.refs_0_, bf16[512,512]{1,0:T(8,128)(2,1)} %get-tuple-element.9.refs_1_, f32[24,512]{1,0:T(8,128)} %get-tuple-element.10.refs_2_, ...), custom_call_target="tpu_custom_call" | custom-call | tf_op jit(solution)/shard_map/pallas_call | solution.py:593

commit v5 on v4

--- a/solution.py
+++ b/solution.py
@@ -13,7 +13,7 @@
 MESH = pl.DeviceIdType.MESH
 F32 = jnp.float32
 BF16 = jnp.bfloat16
-ROWS = 256
+ROWS = 512
 
 
 def dot(a, b):
@@ -70,6 +70,7 @@
                 span = pl.ds(used, max(hops, 1))
                 self.chains.append((half, sign, hops, staged.at[span], slots.at[span]))
                 used += hops
+        self.chains.sort(key=lambda chain: -chain[2])
         self.last = [None] * 4
         self.staged = staged
         self.pairs = {}
@@ -257,6 +258,8 @@
     norm_back,
     pre_back,
     from_sender,
+    scaled_mean,
+    local_rows,
     weight_sq,
     halo_grad,
     returned,
@@ -350,14 +353,17 @@
     inputs_t[pl.ds(0, width)] = jnp.transpose(edge[...])
     from_sender[...] = hot_columns(sender_row, table.shape[0])
     upstream[...] = dot(receiver_hot, cot[...])
+    scaled_mean[...] = jnp.mean(upstream[...] * vectors[2], -1, keepdims=True)
+    local_rows[...] = dot(from_sender[:, pl.ds(0, nodes)], node).astype(BF16)
+    preact[...] += dot(local_rows[...], w_first[pl.ds(width, width)])
     weight_sq[...] = slab_rows(jnp.square(w_first[...].astype(F32)), jnp.square(w_second[...].astype(F32)))
     wait_for(arriving, halo_sem)
     for i in range(edges // ROWS):
         rows = pl.ds(i * ROWS, ROWS)
-        sender_rows = dot(from_sender[rows], table[...]).astype(BF16)
-        inputs_t[pl.ds(width, width), rows] = jnp.transpose(sender_rows)
-        pre = preact[rows] + dot(sender_rows, w_first[pl.ds(width, width)])
-        sigma = 1.0 / (1.0 + jnp.exp(-pre))
+        halo_rows = dot(from_sender[rows, pl.ds(nodes, 4 * slots)], arriving[...]).astype(BF16)
+        inputs_t[pl.ds(width, width), rows] = jnp.transpose(local_rows[rows] + halo_rows)
+        pre = preact[rows] + dot(halo_rows, w_first[pl.ds(width, width)])
+        sigma = 0.5 * jnp.tanh(0.5 * pre) + 0.5
         activation = (pre * sigma).astype(BF16)
         activation_t[:, rows] = jnp.transpose(activation)
         slope = sigma * (1.0 + pre * (1.0 - sigma))
@@ -371,7 +377,7 @@
             inv_std
             * (
                 scaled
-                - jnp.mean(scaled, -1, keepdims=True)
+                - scaled_mean[rows]
                 - normalized * jnp.mean(scaled * normalized, -1, keepdims=True)
             )
         ).astype(BF16)
@@ -476,12 +482,15 @@
 
 def deliver(*refs):
     count = (len(refs) - 2) // 3
-    sources, targets, held = refs[:count], refs[count : 2 * count], refs[2 * count : 3 * count]
     moves = []
-    for i in range(count):
-        load = pltpu.make_async_copy(sources[i], held[i], refs[-2].at[i])
-        load.start()
-        moves.append((load, pltpu.make_async_copy(held[i], targets[i], refs[-1].at[i])))
+    for i in sorted(range(count), key=lambda i: -refs[i].shape[0]):
+        source, target, held = refs[i], refs[count + i], refs[2 * count + i]
+        height = min(128, source.shape[0])
+        for j in range(source.shape[0] // height):
+            rows, k = pl.ds(j * height, height), len(moves)
+            load = pltpu.make_async_copy(source.at[rows], held.at[rows], refs[-2].at[k])
+            load.start()
+            moves.append((load, pltpu.make_async_copy(held.at[rows], target.at[rows], refs[-1].at[k])))
     for load, store in moves:
         load.wait()
         store.start()
@@ -541,6 +550,8 @@
             pltpu.VMEM((edges, width), BF16),
             pltpu.VMEM((edges, width), BF16),
             pltpu.VMEM((edges, table_rows), BF16),
+            pltpu.VMEM((edges, 1), F32),
+            pltpu.VMEM((edges, width), BF16),
             pltpu.VMEM((8, 128), F32),
             pltpu.VMEM((4, slots, width), BF16),
             pltpu.VMEM((4, slots, width), BF16),
@@ -596,7 +607,7 @@
         in_specs=[hbm] * 4,
         out_specs=[hbm] * 4,
         scratch_shapes=[pltpu.VMEM(v.shape, v.dtype) for v in results]
-        + [pltpu.SemaphoreType.DMA((4,))] * 2,
+        + [pltpu.SemaphoreType.DMA((7,))] * 2,
         compiler_params=pltpu.CompilerParams(vmem_limit_bytes=56 << 20),
     )(*results)
 

time: 58.5 us -> 57.1 us (0.976)
  Pallas kernels: 57.6 us -> 56.3 us
    pallas_call x1, Pallas kernels: 55.7 us -> 54.3 us  [per_device(): pl.pallas_call(kernel, out_shape=(jax.ShapeDtypeStruct((nodes, width), BF...]
where the time goes in v5:
time: 57.1 us; the launch traced here: 56.9 us
  Pallas kernels  56.3 us (99%)
  between operations  0.64 us (1%)
    pallas_call x1, Pallas kernels, per_device(): pl.pallas_call(kernel, out_shape=(jax.ShapeDtypeStruct((nodes, width), BF...  54.3 us
    pallas_call x1, Pallas kernels, per_device(): pl.pallas_call(deliver, out_shape=[jax.ShapeDtypeStruct(v.shape, v.dtype)...  1.95 us

profile of v5, /device:TPU:1, one launch (start us, length us, event | category | flops | bytes accessed | tf_op | source)
XLA Modules:
  0.0 56.9 jit_solution(5642206112803967861)
XLA Ops:
  0.6 54.3 %shard_map.138 = (bf16[128,512]{1,0:T(8,128)(2,1)}, bf16[512,512]{1,0:T(8,128)(2,1)}, f32[24,512]{1,0:T(8,128)}, f32[8,512]{1,0:T(8,128)}) custom-call(s32[1,4,64]{2,1,0:T(4,128)} %send_hbm.1, s32[512]{0:T(512)} %sender_hbm.1, s32[512]{0:T(512)} %receiver_hbm.1, bf16[512]{0:T(512)(128)(2,1)} %bias_first_hbm.1, bf16[512]{0:T(512)(128)(2,1)} %bias_second_hbm.1, ...), custom_call_target="tpu_custom_call" | custom-call | tf_op jit(solution)/shard_map/pallas_call | solution.py:523
  55.0 2.0 %shard_map.139 = (bf16[128,512]{1,0:T(8,128)(2,1)}, bf16[512,512]{1,0:T(8,128)(2,1)}, f32[24,512]{1,0:T(8,128)}, f32[8,512]{1,0:T(8,128)}) custom-call(bf16[128,512]{1,0:T(8,128)(2,1)} %get-tuple-element.8.refs_0_, bf16[512,512]{1,0:T(8,128)(2,1)} %get-tuple-element.9.refs_1_, f32[24,512]{1,0:T(8,128)} %get-tuple-element.10.refs_2_, ...), custom_call_target="tpu_custom_call" | custom-call | tf_op jit(solution)/shard_map/pallas_call | solution.py:604

commit v6 on v5

--- a/solution.py
+++ b/solution.py
@@ -434,6 +434,11 @@
     rings[1].finish(over_b, over_sent_b)
     to_z = scatter(comm, "z", lambda peer: over_sent_a.at[peer], cross_a)
     to_y = scatter(comm, "y", lambda peer: over_sent_b.at[peer], cross_b)
+    back_sem, back_group = comm.recv_sem(), comm.group(halo_grad)
+    for k, to in enumerate(
+        (wide_neighbour(-1), wide_neighbour(1), narrow_neighbour(-1), narrow_neighbour(1))
+    ):
+        comm.copy(back_group, halo_grad.at[k], returned.at[k], to, back_sem)
     share[0] = total_of(to_z, over_a[lax.axis_index("z")]).astype(BF16)
     share[1] = total_of(to_y, over_b[lax.axis_index("y")]).astype(BF16)
     here = lax.axis_index("x") * 2 + c
@@ -453,11 +458,6 @@
     square = grads * grads
     squares[0] = slab_rows(square[:cut], square[cut:])
     to_y = scatter(comm, "y", lambda peer: squares.at[0], squares_in.at[pl.ds(0, ny - 1)])
-    back_sem, back_group = comm.recv_sem(), comm.group(halo_grad)
-    for k, to in enumerate(
-        (wide_neighbour(-1), wide_neighbour(1), narrow_neighbour(-1), narrow_neighbour(1))
-    ):
-        comm.copy(back_group, halo_grad.at[k], returned.at[k], to, back_sem)
     squares[1] = total_of(to_y, squares[0])
     to_z = scatter(comm, "z", lambda peer: squares.at[1], squares_in.at[pl.ds(ny - 1, nz - 1)])
     wait_for(returned, back_sem)

time: 57.1 us -> 57 us (level)
  no operation moved by 1% of the time
where the time goes in v6:
time: 57 us; the launch traced here: 56.8 us
  Pallas kernels  56.2 us (99%)
  between operations  0.64 us (1%)
    pallas_call x1, Pallas kernels, per_device(): pl.pallas_call(kernel, out_shape=(jax.ShapeDtypeStruct((nodes, width), BF...  54.3 us
    pallas_call x1, Pallas kernels, per_device(): pl.pallas_call(deliver, out_shape=[jax.ShapeDtypeStruct(v.shape, v.dtype)...  1.95 us

profile of v6, /device:TPU:1, one launch (start us, length us, event | category | flops | bytes accessed | tf_op | source)
XLA Modules:
  0.0 56.8 jit_solution(17019539083820777965)
XLA Ops:
  0.6 54.3 %shard_map.138 = (bf16[128,512]{1,0:T(8,128)(2,1)}, bf16[512,512]{1,0:T(8,128)(2,1)}, f32[24,512]{1,0:T(8,128)}, f32[8,512]{1,0:T(8,128)}) custom-call(s32[1,4,64]{2,1,0:T(4,128)} %send_hbm.1, s32[512]{0:T(512)} %sender_hbm.1, s32[512]{0:T(512)} %receiver_hbm.1, bf16[512]{0:T(512)(128)(2,1)} %bias_first_hbm.1, bf16[512]{0:T(512)(128)(2,1)} %bias_second_hbm.1, ...), custom_call_target="tpu_custom_call" | custom-call | tf_op jit(solution)/shard_map/pallas_call | solution.py:523
  54.9 2.0 %shard_map.139 = (bf16[128,512]{1,0:T(8,128)(2,1)}, bf16[512,512]{1,0:T(8,128)(2,1)}, f32[24,512]{1,0:T(8,128)}, f32[8,512]{1,0:T(8,128)}) custom-call(bf16[128,512]{1,0:T(8,128)(2,1)} %get-tuple-element.8.refs_0_, bf16[512,512]{1,0:T(8,128)(2,1)} %get-tuple-element.9.refs_1_, f32[24,512]{1,0:T(8,128)} %get-tuple-element.10.refs_2_, ...), custom_call_target="tpu_custom_call" | custom-call | tf_op jit(solution)/shard_map/pallas_call | solution.py:604
